TPU v7x, 32 devices: a whole 2x2x4 slice. The times are simulated.
32 devices in a mesh: cells: 8 (over z, y), modes: 4 (over x, core).
Axes of the slice: x: 2, y: 2, z: 4, core: 2. Of those that a mesh axis runs over, the one named last changes fastest.
Arguments:
- theta: float32 [8192, 32], P('modes'), may hold values from -6 to 6
- basis: bfloat16 [16384, 8192], P('cells', 'modes'), may hold values from -0.0625 to 0.0625
- mean_logk: float32 [16384], P('cells'), may hold values from -3 to 3
- face_mult: float32 [3, 16384], P(None, 'cells'), may hold values from 0.3 to 3
- storage: float32 [16384], P('cells'), may hold values from 0.05 to 0.5
- sources: float32 [16384], P('cells'), may hold values from -6 to 6
- obs_data: float32 [16384], P('cells'), may hold values from -6 to 6
- obs_weight: float32 [16384], P('cells'), may hold values from 0.1 to 1
- fault_pairs: int32 [2048, 2], P('cells'), may hold values from 0 to 2047, as said below
- fault_mult: float32 [2048], P('cells'), may hold values from 0.1 to 1
- noise: float32 [8192, 32], P('modes'), may hold values from -6 to 6
Outputs:
- theta_next: float32 [8192, 32], P('modes')
- grad: float32 [8192, 32], P('modes')
- pressure: float32 [32, 16384], P('modes', 'cells')
Inputs may be any that keep to these rules, and one draw needn't show every extreme that they name: `fault_pairs`: each block of 256 slots lists its live connections first; each joins a cell (x, y, z) of the block with (x, y+1, z+s), 1 <= s <= 3; the remaining slots pair a cell with itself. Some block is full in every draw.
All inputs are finite; a program needn't handle non-finite values.
Results may differ from a plain program's by a relative error of at most 0.0047.
Values may be sent and summed in bfloat16 or wider, within the bound.
A program may use at most 64 MiB of HBM per device.

v0:
```python
import functools
import math

import jax
import jax.numpy as jnp
from jax import lax
from jax.experimental import pallas as pl
from jax.experimental.pallas import tpu as pltpu
from jax.sharding import PartitionSpec as P

NY = 32
NZ = 64
SWEEPS = 6


LOW_EIG = 0.1
HIGH_EIG = 1.9
STEP_SIZE = 0.01


def extended(block, sides, width):
    for axis, dim in sides:
        count = lax.axis_size(axis)
        forward = [(i, i + 1) for i in range(count - 1)]
        backward = [(target, source) for source, target in forward]
        low = lax.ppermute(
            lax.slice_in_dim(block, block.shape[dim] - width, None, axis=dim), axis, forward
        )
        high = lax.ppermute(lax.slice_in_dim(block, 0, width, axis=dim), axis, backward)
        block = jnp.concatenate([low, block, high], axis=dim)
    return block


def harmonic(left, right):
    return 2.0 * left * right / (left + right)


def pad_axis(array, axis, before, after):
    widths = [(0, 0)] * array.ndim
    widths[axis] = (before, after)
    return jnp.pad(array, widths)


def transmit(perm_ext, mult_ext, mult_y, mult_z, near_cell, far_cell, fault_mult, depth_y, depth_z):
    chains_n = perm_ext.shape[0]
    layers = perm_ext.shape[1] - 2
    trans_x = harmonic(perm_ext[:, :-1], perm_ext[:, 1:]) * mult_ext[:, :-1]
    perm = perm_ext[:, 1:-1].reshape(chains_n, layers, depth_y, depth_z)
    trans_y = (
        harmonic(perm[:, :, :-1], perm[:, :, 1:])
        * mult_y.reshape(1, layers, depth_y, depth_z)[:, :, :-1]
    )
    trans_z = (
        harmonic(perm[..., :-1], perm[..., 1:])
        * mult_z.reshape(1, layers, depth_y, depth_z)[..., :-1]
    )
    flat = perm.reshape(chains_n, -1)
    live = fault_mult * (near_cell != far_cell).astype(jnp.float32)
    trans_n = harmonic(flat[:, near_cell], flat[:, far_cell]) * live[None]
    return (trans_x, trans_y, trans_z, trans_n)


def diagonal_of(trans, storage, near_cell, far_cell, depth_y, depth_z):
    trans_x, trans_y, trans_z, trans_n = trans
    chains_n = trans_x.shape[0]
    layers = trans_x.shape[1] - 1
    total = (trans_x[:, 1:] + trans_x[:, :-1]).reshape(chains_n, layers, depth_y, depth_z)
    total = total + pad_axis(trans_y, 2, 0, 1) + pad_axis(trans_y, 2, 1, 0)
    total = total + pad_axis(trans_z, 3, 0, 1) + pad_axis(trans_z, 3, 1, 0)
    total = total.reshape(chains_n, -1)
    total = total.at[:, near_cell].add(trans_n).at[:, far_cell].add(trans_n)
    return total + storage[None]


def operate(field_ext, trans, storage, near_cell, far_cell, depth_y, depth_z):
    trans_x, trans_y, trans_z, trans_n = trans
    chains_n = field_ext.shape[0]
    layers = field_ext.shape[1] - 2
    flux_x = trans_x * (field_ext[:, :-1] - field_ext[:, 1:])
    result = (flux_x[:, 1:] - flux_x[:, :-1]).reshape(chains_n, layers, depth_y, depth_z)
    field = field_ext[:, 1:-1].reshape(chains_n, layers, depth_y, depth_z)
    flux_y = trans_y * (field[:, :, :-1] - field[:, :, 1:])
    result = result + pad_axis(flux_y, 2, 0, 1) - pad_axis(flux_y, 2, 1, 0)
    flux_z = trans_z * (field[..., :-1] - field[..., 1:])
    result = result + pad_axis(flux_z, 3, 0, 1) - pad_axis(flux_z, 3, 1, 0)
    result = result.reshape(chains_n, -1)
    flat = field.reshape(chains_n, -1)
    flux_n = trans_n * (flat[:, near_cell] - flat[:, far_cell])
    result = result.at[:, near_cell].add(flux_n).at[:, far_cell].add(-flux_n)
    return result + storage[None] * flat


def solve(rhs, apply_fn, diag):
    center = 0.5 * (HIGH_EIG + LOW_EIG)
    half = 0.5 * (HIGH_EIG - LOW_EIG)
    sigma = center / half
    resid = rhs / diag
    direction = resid / center
    iterate = jnp.zeros_like(rhs)
    rho = jnp.asarray(1.0 / sigma, dtype=rhs.dtype)

    def sweep_step(sweep, carry):
        iterate, resid, direction, rho = carry
        iterate = iterate + direction
        resid = resid - apply_fn(direction) / diag
        rho_next = 1.0 / (2.0 * sigma - rho)
        direction = rho_next * rho * direction + 2.0 * rho_next / half * resid
        return (iterate, resid, direction, rho_next)

    iterate, resid, direction, rho = lax.fori_loop(
        0, SWEEPS, sweep_step, (iterate, resid, direction, rho)
    )
    return iterate + direction


def gradient_of(pres_ext, adj_ext, perm_ext, trans, near_cell, far_cell, depth_y, depth_z):
    trans_x, trans_y, trans_z, trans_n = trans
    chains_n = perm_ext.shape[0]
    layers = perm_ext.shape[1] - 2
    coef_x = (
        -(adj_ext[:, :-1] - adj_ext[:, 1:])
        * (pres_ext[:, :-1] - pres_ext[:, 1:])
        * trans_x
        / (perm_ext[:, :-1] + perm_ext[:, 1:])
    )
    result = coef_x[:, 1:] * perm_ext[:, 2:] + coef_x[:, :-1] * perm_ext[:, :-2]
    result = result.reshape(chains_n, layers, depth_y, depth_z)
    shape4 = (chains_n, layers, depth_y, depth_z)
    perm = perm_ext[:, 1:-1].reshape(shape4)
    pres = pres_ext[:, 1:-1].reshape(shape4)
    adj = adj_ext[:, 1:-1].reshape(shape4)
    coef_y = (
        -(adj[:, :, :-1] - adj[:, :, 1:])
        * (pres[:, :, :-1] - pres[:, :, 1:])
        * trans_y
        / (perm[:, :, :-1] + perm[:, :, 1:])
    )
    result = (
        result
        + pad_axis(coef_y * perm[:, :, 1:], 2, 0, 1)
        + pad_axis(coef_y * perm[:, :, :-1], 2, 1, 0)
    )
    coef_z = (
        -(adj[..., :-1] - adj[..., 1:])
        * (pres[..., :-1] - pres[..., 1:])
        * trans_z
        / (perm[..., :-1] + perm[..., 1:])
    )
    result = (
        result
        + pad_axis(coef_z * perm[..., 1:], 3, 0, 1)
        + pad_axis(coef_z * perm[..., :-1], 3, 1, 0)
    )
    result = result.reshape(chains_n, -1)
    perm_f = perm.reshape(chains_n, -1)
    pres_f = pres.reshape(chains_n, -1)
    adj_f = adj.reshape(chains_n, -1)
    perm_a = perm_f[:, near_cell]
    perm_b = perm_f[:, far_cell]
    coef_n = (
        -(adj_f[:, near_cell] - adj_f[:, far_cell])
        * (pres_f[:, near_cell] - pres_f[:, far_cell])
        * trans_n
        / (perm_a + perm_b)
    )
    return result.at[:, near_cell].add(coef_n * perm_b).at[:, far_cell].add(coef_n * perm_a)


def physics(logk, face_mult, storage, sources, obs_data, obs_weight, fault_pairs, fault_mult):
    chains_n, cells_n = logk.shape
    faces = NY * NZ
    layers = cells_n // faces
    near_cell = fault_pairs[:, 0]
    far_cell = fault_pairs[:, 1]
    perm = jnp.exp(logk).reshape(chains_n, layers, faces)
    stacked = jnp.concatenate([perm, face_mult[0].reshape(1, layers, faces)], 0)
    stacked_ext = extended(stacked, (("cells", 1),), 1)
    perm_ext = stacked_ext[:chains_n]
    mult_ext = stacked_ext[chains_n:]
    trans = transmit(
        perm_ext, mult_ext, face_mult[1], face_mult[2], near_cell, far_cell, fault_mult, NY, NZ
    )
    diag = diagonal_of(trans, storage, near_cell, far_cell, NY, NZ)

    def apply_fn(field):
        field_ext = extended(field.reshape(chains_n, layers, faces), (("cells", 1),), 1)
        return operate(field_ext, trans, storage, near_cell, far_cell, NY, NZ)

    rhs = jnp.broadcast_to(sources[None], (chains_n, cells_n))
    pressure = solve(rhs, apply_fn, diag)
    misfit = obs_weight[None] * (pressure - obs_data[None])
    adjoint = solve(misfit, apply_fn, diag)
    both = jnp.concatenate([pressure, adjoint], 0).reshape(2 * chains_n, layers, faces)
    both_ext = extended(both, (("cells", 1),), 1)
    glogk = gradient_of(
        both_ext[:chains_n], both_ext[chains_n:], perm_ext, trans, near_cell, far_cell, NY, NZ
    )
    return (pressure, glogk)


def body(
    theta,
    basis,
    mean_logk,
    face_mult,
    storage,
    sources,
    obs_data,
    obs_weight,
    fault_pairs,
    fault_mult,
    noise,
):
    chains = theta.shape[1]
    share = chains // lax.axis_size("modes")
    theta_b = theta.astype(jnp.bfloat16)
    local_field = lax.dot_general(
        theta_b, basis, (((0,), (1,)), ((), ())), preferred_element_type=jnp.float32
    )
    partial_field = lax.psum(local_field, "modes")
    logk = mean_logk[None] + partial_field
    pressure, glogk = physics(
        logk, face_mult, storage, sources, obs_data, obs_weight, fault_pairs, fault_mult
    )
    glogk_b = glogk.astype(jnp.bfloat16)
    grad_rows = jnp.dot(glogk_b, basis, preferred_element_type=jnp.float32)
    pressure_out = lax.dynamic_slice_in_dim(pressure, lax.axis_index("modes") * share, share, 0)
    mode_grad = lax.psum(grad_rows, "cells")
    grad = mode_grad.T
    theta_next = theta - STEP_SIZE * (grad + theta) + math.sqrt(2.0 * STEP_SIZE) * noise
    return (theta_next, grad, pressure_out)


LANES = 128
N_EARLY = 5
N_LATE = 2


def chebyshev(rhs, inv, sweep):
    center = 0.5 * (HIGH_EIG + LOW_EIG)
    half = 0.5 * (HIGH_EIG - LOW_EIG)
    sigma = center / half
    resid = [b * v for b, v in zip(rhs, inv)]
    direction = [v * (1.0 / center) for v in resid]
    iterate = None
    rho = 1.0 / sigma
    for _ in range(SWEEPS):
        iterate = direction if iterate is None else [a + b for a, b in zip(iterate, direction)]
        resid = [v - d + s for v, d, s in zip(resid, direction, sweep(direction))]
        rho_next = 1.0 / (2.0 * sigma - rho)
        direction = [
            (rho_next * rho) * d + (2.0 * rho_next / half) * v for d, v in zip(direction, resid)
        ]
        rho = rho_next
    return [a + b for a, b in zip(iterate, direction)]


def chain_physics(nx, rows, logk_of, static_of, fault_row, parts, fault_s, coef, pres_s, before_fields, after_pressure, glogk_s):
    hi_iota = lax.broadcasted_iota(jnp.int32, (rows, LANES), 0)
    lo_iota = lax.broadcasted_iota(jnp.int32, (LANES, LANES), 0)
    for x in range(nx):
        got = None
        for part in range(parts):
            near = fault_row(x, part).astype(jnp.int32)
            shift = fault_row(x, parts + part).astype(jnp.int32) - near - NZ
            lo = (lo_iota == (near & (LANES - 1))).astype(jnp.float32)
            hot = jnp.where(hi_iota == (near >> 7), fault_row(x, 2 * parts + part), 0.0)
            left = jnp.concatenate([jnp.where(shift == s, hot, 0.0) for s in (1, 2, 3)], 0)
            term = lax.dot_general(
                left, lo, (((1,), (1,)), ((), ())),
                precision=lax.Precision.HIGHEST, preferred_element_type=jnp.float32,
            )
            got = term if got is None else got + term
        for s in range(3):
            fault_s[s, pl.ds(x * rows, rows), :] = got[s * rows : (s + 1) * rows]

    before_fields()
    lane = lax.broadcasted_iota(jnp.int32, (nx, LANES), 1)
    xpos = lax.broadcasted_iota(jnp.int32, (nx, LANES), 0)
    low = lane < NZ
    zpos = jnp.where(low, lane, lane - NZ)

    def fwd_lane(v, s):
        return pltpu.roll(v, LANES - s, 1)

    def bwd_lane(v, s):
        return pltpu.roll(v, s, 1)

    def halves(vs):
        return [pltpu.roll(v, NZ, 1) for v in vs]

    def up_y(vs, hs):
        n = len(vs)
        return [jnp.where(low, hs[r], hs[(r + 1) % n]) for r in range(n)]

    def down_y(vs, hs):
        n = len(vs)
        return [jnp.where(low, hs[r - 1], hs[r]) for r in range(n)]

    def ahead(vs, hs=None):
        hs = halves(vs) if hs is None else hs
        wy = up_y(vs, hs)
        return (
            [pltpu.roll(v, nx - 1, 0) for v in vs],
            wy,
            [fwd_lane(v, 1) for v in vs],
            [fwd_lane(w, 1) for w in wy],
            [fwd_lane(w, 2) for w in wy],
            [fwd_lane(w, 3) for w in wy],
        )

    def behind_one(kind, vs):
        if kind == 0:
            return [pltpu.roll(v, 1, 0) for v in vs]
        if kind == 2:
            return [bwd_lane(v, 1) for v in vs]
        wy = down_y(vs, halves(vs))
        return wy if kind == 1 else [bwd_lane(w, kind - 2) for w in wy]

    every = range(rows)
    perm = [jnp.exp(logk_of(r)) for r in every]
    perm_a = ahead(perm)
    zero = jnp.zeros((nx, LANES), jnp.float32)
    diag = [static_of(3, r) for r in every]
    for k in range(6):
        trans = []
        for r in every:
            if k < 3:
                m = static_of(k, r)
            else:
                m = fault_s[k - 3, pl.ds(r, nx, stride=rows), :]
            if k == 0:
                live = xpos < nx - 1
            elif k == 1:
                live = None if r < rows - 1 else low
            elif k == 2:
                live = zpos < NZ - 1
            else:
                live = m > 0.0
            a, b = perm[r], perm_a[k][r]
            total = a + b
            t = 2.0 * a * b / total * m
            if live is not None:
                t = jnp.where(live, t, zero)
            g = t / total
            coef[12 + k, r] = g
            trans.append(t)
        back = behind_one(k, trans)
        for r in every:
            coef[2 * k, r] = trans[r]
            coef[2 * k + 1, r] = back[r]
            diag[r] = diag[r] + trans[r] + back[r]
    inv = [1.0 / v for v in diag]
    for k in range(12):
        for r in every:
            coef[k, r] = coef[k, r] * inv[r]

    def sweep(d):
        hs = halves(d)
        up = up_y(d, hs)
        dn = down_y(d, hs)
        out = []
        for r in every:
            v = d[r]
            acc = coef[0, r] * pltpu.roll(v, nx - 1, 0) + coef[1, r] * pltpu.roll(v, 1, 0)
            acc2 = coef[2, r] * up[r] + coef[3, r] * dn[r]
            acc = acc + coef[4, r] * fwd_lane(v, 1) + coef[5, r] * bwd_lane(v, 1)
            for s in (1, 2, 3):
                acc2 = acc2 + coef[4 + 2 * s, r] * fwd_lane(up[r], s)
                acc = acc + coef[5 + 2 * s, r] * bwd_lane(dn[r], s)
            out.append(acc + acc2)
        return out

    pres = chebyshev([static_of(4, r) for r in every], inv, sweep)
    for r in every:
        pres_s[pl.ds(r, nx, stride=rows), :] = pres[r]
    after_pressure()
    misfit = [static_of(6, r) * (pres[r] - static_of(5, r)) for r in every]
    adj = chebyshev(misfit, inv, sweep)
    pres_a = ahead(pres)
    adj_a = ahead(adj)
    perm_a = ahead(perm)
    total = [zero for r in every]
    for k in range(6):
        q = [
            -(adj[r] - adj_a[k][r]) * (pres[r] - pres_a[k][r]) * coef[12 + k, r] for r in every
        ]
        back = behind_one(k, [q[r] * perm[r] for r in every])
        for r in every:
            total[r] = total[r] + q[r] * perm_a[k][r] + back[r]
    for r in every:
        glogk_s[pl.ds(r, nx, stride=rows), :] = total[r]


def fused_kernel(
    nd, nm, rows, stat_rows, parts, axes,
    theta_ref, basis_hbm, mean_ref, face_ref, storage_ref, sources_ref, data_ref, weight_ref,
    pairs_ref, mult_ref,
    grad_out, pres_out,
    basis, stat_all, late_all, part, part_in, mine, field, fault_s, coef, pres_s, pres_in,
    glogk_s, gl_b, gl_all, gl_f, gsend, gin, gfin, gall, copy_sem, send_sem, recv_sem,
):
    cells_ax, modes_ax = axes
    me, mo = lax.axis_index(cells_ax), lax.axis_index(modes_ax)
    chains, modes_n = theta_ref.shape
    cells = rows * LANES
    blk = cells // nd
    loads = [
        pltpu.make_async_copy(
            basis_hbm.at[pl.ds(k * blk, blk)], basis.at[pl.ds(k * blk, blk)], copy_sem.at[k]
        )
        for k in range(nd)
    ]
    for load in loads:
        load.start()

    def cell_peer(k):
        return {cells_ax: lax.rem(me + k, nd)}

    def mode_peer(k):
        return {modes_ax: lax.rem(mo + k, nm)}

    barrier = pltpu.get_barrier_semaphore()
    for k in range(1, nd):
        pl.semaphore_signal(
            barrier, inc=1, device_id=cell_peer(k), device_id_type=pl.DeviceIdType.MESH
        )
    for k in range(1, nm):
        pl.semaphore_signal(
            barrier, inc=1, device_id=mode_peer(k), device_id_type=pl.DeviceIdType.MESH
        )
    sent = []
    count = [0]

    def send(src, dst, peer):
        slot = count[0]
        count[0] += 1
        copy = pltpu.make_async_remote_copy(
            src_ref=src, dst_ref=dst, send_sem=send_sem.at[slot], recv_sem=recv_sem.at[slot],
            device_id=peer, device_id_type=pl.DeviceIdType.MESH,
        )
        copy.start()
        sent.append(copy)
        return copy

    def block(i, size):
        return pl.ds(pl.multiple_of(i * size, size), size)

    def peer_of(k):
        return lax.rem(me + k, nd)

    base = pl.multiple_of(me * stat_rows, 8)
    for f in range(face_ref.shape[0]):
        stat_all[pl.ds(base + f * rows, rows), :] = jnp.concatenate(
            [face_ref[f : f + 1, r * LANES : (r + 1) * LANES] for r in range(rows)], 0
        )
    stat_all[pl.ds(base + 3 * rows, rows), :] = storage_ref[...]
    stat_all[pl.ds(base + 4 * rows, rows), :] = sources_ref[...]
    pairs = pairs_ref[...].astype(jnp.float32)
    spare = stat_rows - N_EARLY * rows - 3 * parts
    stat_all[pl.ds(base + N_EARLY * rows, stat_rows - N_EARLY * rows), :] = jnp.concatenate(
        [pairs[e : e + 1, p * LANES : (p + 1) * LANES] for e in range(2) for p in range(parts)]
        + [mult_ref[...]]
        + ([jnp.zeros((spare, LANES), jnp.float32)] if spare else []),
        0,
    )
    late_rows = N_LATE * rows
    late_base = pl.multiple_of(me * late_rows, 8)
    late_all[pl.ds(late_base, rows), :] = data_ref[...]
    late_all[pl.ds(late_base + rows, rows), :] = weight_ref[...]

    theta_b = theta_ref[...].astype(jnp.bfloat16)
    own = nd * rows
    half = rows // 2
    lead = 1
    stat_got, part_got = [], [[], []]
    for k in range(nd):
        loads[k].wait()
        got = lax.dot_general(
            theta_b, basis[pl.ds(k * blk, blk), :], (((1,), (1,)), ((), ())),
            preferred_element_type=jnp.float32,
        )
        for t in range(blk // LANES):
            r = k * (blk // LANES) + t
            part[r // half, pl.ds(r % half, chains, stride=half), :] = (
                got[:, t * LANES : (t + 1) * LANES]
            )
        if k == lead - 1:
            pl.semaphore_wait(barrier, nd + nm - 2)
            stat_got = [
                send(
                    stat_all.at[block(me, stat_rows)], stat_all.at[block(me, stat_rows)],
                    cell_peer(j),
                )
                for j in range(1, nd)
            ]
        if (k + 1) % (nd // 2) == 0:
            h = k // (nd // 2)
            for j in range(1, nm):
                src = part.at[h, block(lax.rem(mo + j, nm), nd * half)]
                part_got[h].append(send(src, part_in.at[h, j - 1], mode_peer(j)))
    mean = mean_ref[...]
    for h in range(2):
        total = part[h, block(mo, nd * half), :].reshape(nd, half, LANES)
        total = total + mean[h * half : (h + 1) * half][None]
        for k in range(1, nm):
            part_got[h][k - 1].wait_recv()
            total = total + part_in[h, k - 1].reshape(nd, half, LANES)
        mine[:, h * half : (h + 1) * half, :] = total
    field_got = [
        send(mine.at[peer_of(k)], field.at[block(me, rows)], cell_peer(k))
        for k in range(1, nd)
    ]
    field[block(me, rows), :] = mine[me]
    late_got = [
        send(
            late_all.at[block(me, late_rows)], late_all.at[block(me, late_rows)], cell_peer(k)
        )
        for k in range(1, nd)
    ]
    for copy in stat_got:
        copy.wait_recv()

    def before_fields():
        for copy in field_got:
            copy.wait_recv()

    def static_of(f, r):
        if f >= N_EARLY:
            return late_all[pl.ds((f - N_EARLY) * rows + r, nd, stride=late_rows), :]
        return stat_all[pl.ds(f * rows + r, nd, stride=stat_rows), :]

    def logk_of(r):
        return field[pl.ds(r, nd, stride=rows), :]

    def fault_row(x, k):
        return stat_all[pl.ds(x * stat_rows + N_EARLY * rows + k, 1), :]

    pres_got = []

    def after_pressure():
        for k in range(1, nd):
            pres_got.append(
                send(pres_s.at[block(peer_of(k), rows)], pres_in.at[block(me, rows)], cell_peer(k))
            )
        pres_in[block(me, rows), :] = pres_s[block(me, rows), :]
        for copy in late_got:
            copy.wait_recv()

    chain_physics(
        nd, rows, logk_of, static_of, fault_row, parts, fault_s, coef, pres_s, before_fields,
        after_pressure, glogk_s,
    )

    gl_b[...] = glogk_s[...].astype(jnp.bfloat16)
    spot = block(mo * nd + me, rows)
    gl_got = [
        send(gl_b.at[block(peer_of(k), rows)], gl_all.at[spot], cell_peer(k)) for k in range(1, nd)
    ]
    gl_all[spot, :] = gl_b[block(me, rows), :]
    for copy in gl_got:
        copy.wait_recv()
    spot = block(mo, own)
    gl_got = [send(gl_all.at[spot], gl_all.at[spot], mode_peer(k)) for k in range(1, nm)]
    for copy in pres_got:
        copy.wait_recv()
    pres_out[...] = pres_in[...]
    for copy in gl_got:
        copy.wait_recv()
    gl_f[...] = gl_all[...].astype(jnp.float32)
    glogk = jnp.concatenate(
        [gl_f[pl.ds(r, chains, stride=rows), :] for r in range(rows)], 1
    ).astype(jnp.bfloat16)

    width = modes_n // nd

    def piece(k):
        return jnp.dot(
            glogk, basis[:, block(peer_of(k), width)], preferred_element_type=jnp.float32
        )

    g_got = []
    for k in range(1, nd):
        gsend[k - 1] = piece(k).astype(jnp.bfloat16)
        g_got.append(send(gsend.at[k - 1], gin.at[k - 1], cell_peer(k)))
    grad = piece(0)
    for k in range(1, nd):
        g_got[k - 1].wait_recv()
        grad = grad + gin[k - 1].astype(jnp.float32)
    gfin[...] = grad.astype(jnp.bfloat16)
    g_got = [send(gfin, gall.at[me], cell_peer(k)) for k in range(1, nd)]
    gall[me] = gfin[...]
    for copy in g_got:
        copy.wait_recv()
    grad_out[...] = gall[...]
    for copy in sent:
        copy.wait_send()


def finish_kernel(grad_ref, pres_ref, theta_ref, noise_ref, theta_out, grad_out, pres_out):
    pieces, _, width = grad_ref.shape
    for p in range(pieces):
        cols = slice(p * width, (p + 1) * width)
        g = grad_ref[p].astype(jnp.float32)
        t = theta_ref[:, cols]
        grad_out[:, cols] = g
        theta_out[:, cols] = (
            t - STEP_SIZE * (g + t) + math.sqrt(2.0 * STEP_SIZE) * noise_ref[:, cols]
        )
    count = pres_out.shape[0]
    rows = pres_out.shape[1] // LANES
    for r in range(rows):
        pres_out[:, r * LANES : (r + 1) * LANES] = pres_ref[pl.ds(r, count, stride=rows), :]


def fast_body(
    theta, basis, mean_logk, face_mult, storage, sources, obs_data, obs_weight,
    fault_pairs, fault_mult, noise,
):
    nd, nm = lax.axis_size("cells"), lax.axis_size("modes")
    cells, modes_n = basis.shape
    chains = theta.shape[1]
    rows = cells // LANES
    parts = fault_mult.shape[0] // LANES
    stat_rows = N_EARLY * rows + -(-3 * parts // 8) * 8
    f32, bf16 = jnp.float32, jnp.bfloat16
    width = modes_n // nd
    copies = 7 * (nd - 1) + 3 * (nm - 1)
    vmem = pl.BlockSpec(memory_space=pltpu.VMEM)
    grad, pressure = pl.pallas_call(
        functools.partial(fused_kernel, nd, nm, rows, stat_rows, parts, ("cells", "modes")),
        out_shape=(
            jax.ShapeDtypeStruct((nd, chains, width), bf16),
            jax.ShapeDtypeStruct((nd * rows, LANES), f32),
        ),
        in_specs=[vmem, pl.BlockSpec(memory_space=pl.ANY)] + [vmem] * 8,
        out_specs=(vmem,) * 2,
        scratch_shapes=[
            pltpu.VMEM((cells, modes_n), bf16),
            pltpu.VMEM((nd * stat_rows, LANES), f32),
            pltpu.VMEM((nd * N_LATE * rows, LANES), f32),
            pltpu.VMEM((2, chains * rows // 2, LANES), f32),
            pltpu.VMEM((2, nm - 1, nd * rows // 2, LANES), f32),
            pltpu.VMEM((nd, rows, LANES), f32),
            pltpu.VMEM((nd * rows, LANES), f32),
            pltpu.VMEM((3, nd * rows, LANES), f32),
            pltpu.VMEM((18, rows, nd, LANES), f32),
            pltpu.VMEM((nd * rows, LANES), f32),
            pltpu.VMEM((nd * rows, LANES), f32),
            pltpu.VMEM((nd * rows, LANES), f32),
            pltpu.VMEM((nd * rows, LANES), bf16),
            pltpu.VMEM((chains * rows, LANES), bf16),
            pltpu.VMEM((chains * rows, LANES), f32),
            pltpu.VMEM((nd - 1, chains, width), bf16),
            pltpu.VMEM((nd - 1, chains, width), bf16),
            pltpu.VMEM((chains, width), bf16),
            pltpu.VMEM((nd, chains, width), bf16),
            pltpu.SemaphoreType.DMA((nd,)),
            pltpu.SemaphoreType.DMA((copies,)),
            pltpu.SemaphoreType.DMA((copies,)),
        ],
        compiler_params=pltpu.CompilerParams(collective_id=0, has_side_effects=True),
    )(
        theta.T, basis, mean_logk.reshape(-1, LANES), face_mult, storage.reshape(-1, LANES),
        sources.reshape(-1, LANES), obs_data.reshape(-1, LANES), obs_weight.reshape(-1, LANES),
        fault_pairs.T, fault_mult.reshape(-1, LANES),
    )
    theta_next, grad, pressure = pl.pallas_call(
        finish_kernel,
        out_shape=(
            jax.ShapeDtypeStruct((chains, modes_n), f32),
            jax.ShapeDtypeStruct((chains, modes_n), f32),
            jax.ShapeDtypeStruct((chains // nm, cells), f32),
        ),
        in_specs=[vmem] * 4,
        out_specs=(vmem,) * 3,
    )(grad, pressure, theta.T, noise.T)
    return (theta_next.T, grad.T, pressure)


def choose_body(theta, basis, *rest):
    share = theta.shape[1] // lax.axis_size("modes")
    nx = lax.axis_size("cells")
    whole = basis.shape[0] == NY * NZ and rest[-2].shape[0] % LANES == 0 and 2 * NZ == LANES
    if share == nx and nx == 8 and whole and basis.shape[1] % (nx * LANES) == 0:
        return fast_body(theta, basis, *rest)
    return body(theta, basis, *rest)


def solution(mesh):
    return jax.shard_map(
        choose_body,
        mesh=mesh,
        in_specs=(
            P("modes", None),
            P("cells", "modes"),
            P("cells"),
            P(None, "cells"),
            P("cells"),
            P("cells"),
            P("cells"),
            P("cells"),
            P("cells", None),
            P("cells"),
            P("modes", None),
        ),
        out_specs=(P("modes", None), P("modes", None), P("modes", "cells")),
        check_vma=False,
    )
```

profile of v0, /device:TPU:0, one launch (start us, length us, event | category | flops | bytes accessed | tf_op | source)
XLA Modules:
  0.0 45.7 jit_solution(16291638248701471698)
XLA Ops:
  0.6 43.1 %shard_map.130 = (bf16[8,32,256]{2,1,0:T(8,128)(2,1)}, f32[128,128]{1,0:T(8,128)}) custom-call(f32[32,2048]{1,0:T(8,128)} %bitcast.11, bf16[2048,2048]{1,0:T(8,128)(2,1)} %basis_hbm.1, f32[16,128]{1,0:T(8,128)} %bitcast.14, f32[3,2048]{1,0:T(4,128)} %face_ref.1, f32[16,128]{1,0:T(8,128)} %bitcast.15, f32[16,128]{1,0:T(8,128)} %bitcast.16, ...), custom_call_target="tpu_custom_call" | custom-call | tf_op jit(solution)/shard_map/pallas_call | solution.py:630
  43.7 2.0 %shard_map.131 = (f32[32,2048]{1,0:T(8,128)}, f32[32,2048]{1,0:T(8,128)}, f32[8,2048]{1,0:T(8,128)}) custom-call(bf16[8,32,256]{2,1,0:T(8,128)(2,1)} %get-tuple-element.8.grad_ref, f32[128,128]{1,0:T(8,128)} %get-tuple-element.9.pres_ref, f32[32,2048]{1,0:T(8,128)} %bitcast.12, f32[32,2048]{1,0:T(8,128)} %bitcast.13), custom_call_target="tpu_custom_call" | custom-call | tf_op jit(solution)/shard_map/pallas_call | solution.py:668
where the time goes:
time: 45.9 us; the launch traced here: 45.7 us
  Pallas kernels  45.1 us (98%)
  between operations  0.64 us (1%)
    pallas_call x1, Pallas kernels, fast_body(): pl.pallas_call(functools.partial(fused_kernel, nd, nm, rows, stat_rows, p...  43.1 us
    pallas_call x1, Pallas kernels, fast_body(): pl.pallas_call(finish_kernel, out_shape=(jax.ShapeDtypeStruct((chains, mo...  1.99 us

commit v1 on v0

--- a/solution.py
+++ b/solution.py
@@ -232,8 +232,7 @@
 
 
 LANES = 128
-N_EARLY = 5
-N_LATE = 2
+STAT = 4
 
 
 def chebyshev(rhs, inv, sweep):
@@ -393,42 +392,72 @@
 
 
 def fused_kernel(
-    nd, nm, rows, stat_rows, parts, axes,
-    theta_ref, basis_hbm, mean_ref, face_ref, storage_ref, sources_ref, data_ref, weight_ref,
-    pairs_ref, mult_ref,
+    nd, nm, rows, parts, axes,
+    theta_hbm, basis_hbm, mean_hbm, face_hbm, storage_hbm, sources_hbm, data_hbm, weight_hbm,
+    pairs_hbm, mult_hbm,
     grad_out, pres_out,
-    basis, stat_all, late_all, part, part_in, mine, field, fault_s, coef, pres_s, pres_in,
-    glogk_s, gl_b, gl_all, gl_f, gsend, gin, gfin, gall, copy_sem, send_sem, recv_sem,
+    basis, theta_v, mean_v, face_v, pairs_v, mult_v, own_stat, stat, part, part_in, mine, field,
+    fault_s, coef, pres_s, pres_in, glogk_s, gl_b, gl_all, gl_f, gsend, gin, gfin, gall,
+    load_sem, copy_sem, send_sem, recv_sem,
 ):
     cells_ax, modes_ax = axes
     me, mo = lax.axis_index(cells_ax), lax.axis_index(modes_ax)
-    chains, modes_n = theta_ref.shape
+    chains, modes_n = theta_v.shape
     cells = rows * LANES
     blk = cells // nd
+    pairs_n = nm // 2
+    core, group = lax.rem(mo, 2), lax.div(mo, 2)
+    high, low = lax.div(me, 2), lax.rem(me, 2)
+    srows = STAT * rows
+    small = [
+        (theta_hbm, theta_v),
+        (face_hbm, face_v),
+        (storage_hbm, own_stat.at[0, pl.ds(3 * rows, rows)]),
+        (sources_hbm, own_stat.at[1, pl.ds(0, rows)]),
+        (data_hbm, own_stat.at[1, pl.ds(rows, rows)]),
+        (weight_hbm, own_stat.at[1, pl.ds(2 * rows, rows)]),
+        (pairs_hbm, pairs_v),
+        (mult_hbm, mult_v),
+        (mean_hbm, mean_v),
+    ]
+    small = [pltpu.make_async_copy(a, b, load_sem.at[i]) for i, (a, b) in enumerate(small)]
     loads = [
         pltpu.make_async_copy(
             basis_hbm.at[pl.ds(k * blk, blk)], basis.at[pl.ds(k * blk, blk)], copy_sem.at[k]
         )
         for k in range(nd)
     ]
-    for load in loads:
+    for load in small + loads:
         load.start()
 
-    def cell_peer(k):
-        return {cells_ax: lax.rem(me + k, nd)}
-
-    def mode_peer(k):
-        return {modes_ax: lax.rem(mo + k, nm)}
+    def block(i, size):
+        return pl.ds(pl.multiple_of(i * size, size), size)
+
+    steps = sorted(
+        ((dz, dy) for dz in range(nd // 2) for dy in range(2)),
+        key=lambda t: -(min(t[0], nd // 2 - t[0]) + t[1]),
+    )
+
+    def cell_of(step):
+        return lax.rem(high + step[0], nd // 2) * 2 + lax.rem(low + step[1], 2)
+
+    near = [t for t in steps if t != (0, 0)]
+    wide = sorted(
+        ((t, dx) for t in steps for dx in range(pairs_n) if (t, dx) != ((0, 0), 0)),
+        key=lambda w: -(min(w[0][0], nd // 2 - w[0][0]) + w[0][1] + (w[1] > 0)),
+    )
+    mate = {modes_ax: group * 2 + 1 - core}
+
+    def group_of(dx):
+        return lax.rem(group + dx, pairs_n)
+
+    def wide_peer(t, dx):
+        return {cells_ax: cell_of(t), modes_ax: group_of(dx) * 2 + core}
 
     barrier = pltpu.get_barrier_semaphore()
-    for k in range(1, nd):
-        pl.semaphore_signal(
-            barrier, inc=1, device_id=cell_peer(k), device_id_type=pl.DeviceIdType.MESH
-        )
-    for k in range(1, nm):
-        pl.semaphore_signal(
-            barrier, inc=1, device_id=mode_peer(k), device_id_type=pl.DeviceIdType.MESH
-        )
+    for peer in [wide_peer(t, dx) for t, dx in wide] + [mate]:
+        pl.semaphore_signal(barrier, inc=1, device_id=peer, device_id_type=pl.DeviceIdType.MESH)
+    greeted = len(wide) + 1
     sent = []
     count = [0]
 
@@ -443,109 +472,103 @@
         sent.append(copy)
         return copy
 
-    def block(i, size):
-        return pl.ds(pl.multiple_of(i * size, size), size)
-
-    def peer_of(k):
-        return lax.rem(me + k, nd)
-
-    base = pl.multiple_of(me * stat_rows, 8)
-    for f in range(face_ref.shape[0]):
-        stat_all[pl.ds(base + f * rows, rows), :] = jnp.concatenate(
-            [face_ref[f : f + 1, r * LANES : (r + 1) * LANES] for r in range(rows)], 0
-        )
-    stat_all[pl.ds(base + 3 * rows, rows), :] = storage_ref[...]
-    stat_all[pl.ds(base + 4 * rows, rows), :] = sources_ref[...]
-    pairs = pairs_ref[...].astype(jnp.float32)
-    spare = stat_rows - N_EARLY * rows - 3 * parts
-    stat_all[pl.ds(base + N_EARLY * rows, stat_rows - N_EARLY * rows), :] = jnp.concatenate(
+    def cell_peer(t):
+        return {cells_ax: cell_of(t)}
+
+    for load in small:
+        load.wait()
+    for f in range(3):
+        own_stat[0, f * rows : (f + 1) * rows, :] = jnp.concatenate(
+            [face_v[f : f + 1, r * LANES : (r + 1) * LANES] for r in range(rows)], 0
+        )
+    pairs = pairs_v[...].astype(jnp.float32)
+    spare = rows - 3 * parts
+    own_stat[1, 3 * rows :, :] = jnp.concatenate(
         [pairs[e : e + 1, p * LANES : (p + 1) * LANES] for e in range(2) for p in range(parts)]
-        + [mult_ref[...]]
+        + [mult_v[...]]
         + ([jnp.zeros((spare, LANES), jnp.float32)] if spare else []),
         0,
     )
-    late_rows = N_LATE * rows
-    late_base = pl.multiple_of(me * late_rows, 8)
-    late_all[pl.ds(late_base, rows), :] = data_ref[...]
-    late_all[pl.ds(late_base + rows, rows), :] = weight_ref[...]
-
-    theta_b = theta_ref[...].astype(jnp.bfloat16)
-    own = nd * rows
+    stat[core, block(me, srows), :] = own_stat[core]
+    share = chains // nm
+    theta_t = jnp.concatenate(
+        [
+            theta_v[(2 * x + c) * share : (2 * x + c + 1) * share, :]
+            for c in range(2)
+            for x in range(pairs_n)
+        ],
+        0,
+    ).T.astype(jnp.bfloat16)
     half = rows // 2
     lead = 1
-    stat_got, part_got = [], [[], []]
+    stat_got, part_got = [], []
     for k in range(nd):
         loads[k].wait()
-        got = lax.dot_general(
-            theta_b, basis[pl.ds(k * blk, blk), :], (((1,), (1,)), ((), ())),
-            preferred_element_type=jnp.float32,
-        )
+        got = jnp.dot(
+            basis[pl.ds(k * blk, blk), :], theta_t, preferred_element_type=jnp.float32
+        ).T
         for t in range(blk // LANES):
             r = k * (blk // LANES) + t
             part[r // half, pl.ds(r % half, chains, stride=half), :] = (
                 got[:, t * LANES : (t + 1) * LANES]
             )
         if k == lead - 1:
-            pl.semaphore_wait(barrier, nd + nm - 2)
+            pl.semaphore_wait(barrier, greeted)
             stat_got = [
-                send(
-                    stat_all.at[block(me, stat_rows)], stat_all.at[block(me, stat_rows)],
-                    cell_peer(j),
-                )
-                for j in range(1, nd)
+                send(own_stat.at[core], stat.at[core, block(me, srows)], cell_peer(t))
+                for t in near
             ]
         if (k + 1) % (nd // 2) == 0:
             h = k // (nd // 2)
-            for j in range(1, nm):
-                src = part.at[h, block(lax.rem(mo + j, nm), nd * half)]
-                part_got[h].append(send(src, part_in.at[h, j - 1], mode_peer(j)))
-    mean = mean_ref[...]
+            part_got.append(
+                send(part.at[h, block(1 - core, chains // 2 * half)], part_in.at[h], mate)
+            )
+    mean = 1.0 / pairs_n * mean_v[...]
     for h in range(2):
-        total = part[h, block(mo, nd * half), :].reshape(nd, half, LANES)
+        total = part[h, block(core, chains // 2 * half), :].reshape(chains // 2, half, LANES)
         total = total + mean[h * half : (h + 1) * half][None]
-        for k in range(1, nm):
-            part_got[h][k - 1].wait_recv()
-            total = total + part_in[h, k - 1].reshape(nd, half, LANES)
+        part_got[h].wait_recv()
+        total = total + part_in[h].reshape(chains // 2, half, LANES)
         mine[:, h * half : (h + 1) * half, :] = total
     field_got = [
-        send(mine.at[peer_of(k)], field.at[block(me, rows)], cell_peer(k))
-        for k in range(1, nd)
+        send(
+            mine.at[group_of(dx) * nd + cell_of(t)], field.at[group, block(me, rows)],
+            wide_peer(t, dx),
+        )
+        for t, dx in wide
     ]
-    field[block(me, rows), :] = mine[me]
-    late_got = [
-        send(
-            late_all.at[block(me, late_rows)], late_all.at[block(me, late_rows)], cell_peer(k)
-        )
-        for k in range(1, nd)
-    ]
+    field[group, block(me, rows), :] = mine[group * nd + me]
     for copy in stat_got:
         copy.wait_recv()
+    send(stat.at[core], stat.at[core], mate).wait_recv()
 
     def before_fields():
         for copy in field_got:
             copy.wait_recv()
 
     def static_of(f, r):
-        if f >= N_EARLY:
-            return late_all[pl.ds((f - N_EARLY) * rows + r, nd, stride=late_rows), :]
-        return stat_all[pl.ds(f * rows + r, nd, stride=stat_rows), :]
+        h, f = (0, f) if f < STAT else (1, f - STAT)
+        return stat[h, pl.ds(f * rows + r, nd, stride=srows), :]
 
     def logk_of(r):
-        return field[pl.ds(r, nd, stride=rows), :]
+        value = field[0, pl.ds(r, nd, stride=rows), :]
+        for g in range(1, pairs_n):
+            value = value + field[g, pl.ds(r, nd, stride=rows), :]
+        return value
 
     def fault_row(x, k):
-        return stat_all[pl.ds(x * stat_rows + N_EARLY * rows + k, 1), :]
+        return stat[1, pl.ds(x * srows + 3 * rows + k, 1), :]
 
     pres_got = []
 
     def after_pressure():
-        for k in range(1, nd):
+        for t in near:
             pres_got.append(
-                send(pres_s.at[block(peer_of(k), rows)], pres_in.at[block(me, rows)], cell_peer(k))
+                send(
+                    pres_s.at[block(cell_of(t), rows)], pres_in.at[block(me, rows)], cell_peer(t)
+                )
             )
         pres_in[block(me, rows), :] = pres_s[block(me, rows), :]
-        for copy in late_got:
-            copy.wait_recv()
 
     chain_physics(
         nd, rows, logk_of, static_of, fault_row, parts, fault_s, coef, pres_s, before_fields,
@@ -553,42 +576,43 @@
     )
 
     gl_b[...] = glogk_s[...].astype(jnp.bfloat16)
-    spot = block(mo * nd + me, rows)
+    spot = block(group * nd + me, rows)
     gl_got = [
-        send(gl_b.at[block(peer_of(k), rows)], gl_all.at[spot], cell_peer(k)) for k in range(1, nd)
+        send(gl_b.at[block(cell_of(t), rows)], gl_all.at[core, spot], wide_peer(t, dx))
+        for t, dx in wide
     ]
-    gl_all[spot, :] = gl_b[block(me, rows), :]
+    gl_all[core, spot, :] = gl_b[block(me, rows), :]
     for copy in gl_got:
         copy.wait_recv()
-    spot = block(mo, own)
-    gl_got = [send(gl_all.at[spot], gl_all.at[spot], mode_peer(k)) for k in range(1, nm)]
+    mate_got = send(gl_all.at[core], gl_all.at[core], mate)
     for copy in pres_got:
         copy.wait_recv()
     pres_out[...] = pres_in[...]
-    for copy in gl_got:
-        copy.wait_recv()
-    gl_f[...] = gl_all[...].astype(jnp.float32)
+    mate_got.wait_recv()
+    held = chains // 2 * rows
+    for c in range(2):
+        gl_f[c * held : (c + 1) * held, :] = gl_all[c].astype(jnp.float32)
     glogk = jnp.concatenate(
         [gl_f[pl.ds(r, chains, stride=rows), :] for r in range(rows)], 1
     ).astype(jnp.bfloat16)
 
     width = modes_n // nd
 
-    def piece(k):
+    def piece(i):
         return jnp.dot(
-            glogk, basis[:, block(peer_of(k), width)], preferred_element_type=jnp.float32
+            glogk, basis[:, block(i, width)], preferred_element_type=jnp.float32
         )
 
     g_got = []
-    for k in range(1, nd):
-        gsend[k - 1] = piece(k).astype(jnp.bfloat16)
-        g_got.append(send(gsend.at[k - 1], gin.at[k - 1], cell_peer(k)))
-    grad = piece(0)
-    for k in range(1, nd):
-        g_got[k - 1].wait_recv()
-        grad = grad + gin[k - 1].astype(jnp.float32)
+    for k, t in enumerate(near):
+        gsend[k] = piece(cell_of(t)).astype(jnp.bfloat16)
+        g_got.append(send(gsend.at[k], gin.at[k], cell_peer(t)))
+    grad = piece(me)
+    for k, copy in enumerate(g_got):
+        copy.wait_recv()
+        grad = grad + gin[k].astype(jnp.float32)
     gfin[...] = grad.astype(jnp.bfloat16)
-    g_got = [send(gfin, gall.at[me], cell_peer(k)) for k in range(1, nd)]
+    g_got = [send(gfin, gall.at[me], cell_peer(t)) for t in near]
     gall[me] = gfin[...]
     for copy in g_got:
         copy.wait_recv()
@@ -597,11 +621,16 @@
         copy.wait_send()
 
 
-def finish_kernel(grad_ref, pres_ref, theta_ref, noise_ref, theta_out, grad_out, pres_out):
-    pieces, _, width = grad_ref.shape
+def finish_kernel(nm, grad_ref, pres_ref, theta_ref, noise_ref, theta_out, grad_out, pres_out):
+    pieces, chains, width = grad_ref.shape
+    share = chains // nm
+    order = [x * 2 + c for c in range(2) for x in range(nm // 2)]
     for p in range(pieces):
         cols = slice(p * width, (p + 1) * width)
-        g = grad_ref[p].astype(jnp.float32)
+        piece = grad_ref[p].astype(jnp.float32)
+        g = jnp.concatenate(
+            [piece[order.index(n) * share : (order.index(n) + 1) * share] for n in range(nm)], 0
+        )
         t = theta_ref[:, cols]
         grad_out[:, cols] = g
         theta_out[:, cols] = (
@@ -622,39 +651,45 @@
     chains = theta.shape[1]
     rows = cells // LANES
     parts = fault_mult.shape[0] // LANES
-    stat_rows = N_EARLY * rows + -(-3 * parts // 8) * 8
     f32, bf16 = jnp.float32, jnp.bfloat16
     width = modes_n // nd
-    copies = 7 * (nd - 1) + 3 * (nm - 1)
+    pairs_n = nm // 2
+    copies = 4 * (nd - 1) + 2 * (pairs_n * nd - 1) + 4
     vmem = pl.BlockSpec(memory_space=pltpu.VMEM)
     grad, pressure = pl.pallas_call(
-        functools.partial(fused_kernel, nd, nm, rows, stat_rows, parts, ("cells", "modes")),
+        functools.partial(fused_kernel, nd, nm, rows, parts, ("cells", "modes")),
         out_shape=(
             jax.ShapeDtypeStruct((nd, chains, width), bf16),
             jax.ShapeDtypeStruct((nd * rows, LANES), f32),
         ),
-        in_specs=[vmem, pl.BlockSpec(memory_space=pl.ANY)] + [vmem] * 8,
+        in_specs=[pl.BlockSpec(memory_space=pl.ANY)] * 10,
         out_specs=(vmem,) * 2,
         scratch_shapes=[
             pltpu.VMEM((cells, modes_n), bf16),
-            pltpu.VMEM((nd * stat_rows, LANES), f32),
-            pltpu.VMEM((nd * N_LATE * rows, LANES), f32),
+            pltpu.VMEM((chains, modes_n), f32),
+            pltpu.VMEM((rows, LANES), f32),
+            pltpu.VMEM((3, cells), f32),
+            pltpu.VMEM((2, parts * LANES), jnp.int32),
+            pltpu.VMEM((parts, LANES), f32),
+            pltpu.VMEM((2, STAT * rows, LANES), f32),
+            pltpu.VMEM((2, nd * STAT * rows, LANES), f32),
             pltpu.VMEM((2, chains * rows // 2, LANES), f32),
-            pltpu.VMEM((2, nm - 1, nd * rows // 2, LANES), f32),
-            pltpu.VMEM((nd, rows, LANES), f32),
-            pltpu.VMEM((nd * rows, LANES), f32),
+            pltpu.VMEM((2, chains // 2 * rows // 2, LANES), f32),
+            pltpu.VMEM((pairs_n * nd, rows, LANES), f32),
+            pltpu.VMEM((pairs_n, nd * rows, LANES), f32),
             pltpu.VMEM((3, nd * rows, LANES), f32),
             pltpu.VMEM((18, rows, nd, LANES), f32),
             pltpu.VMEM((nd * rows, LANES), f32),
             pltpu.VMEM((nd * rows, LANES), f32),
             pltpu.VMEM((nd * rows, LANES), f32),
             pltpu.VMEM((nd * rows, LANES), bf16),
-            pltpu.VMEM((chains * rows, LANES), bf16),
+            pltpu.VMEM((2, chains // 2 * rows, LANES), bf16),
             pltpu.VMEM((chains * rows, LANES), f32),
             pltpu.VMEM((nd - 1, chains, width), bf16),
             pltpu.VMEM((nd - 1, chains, width), bf16),
             pltpu.VMEM((chains, width), bf16),
             pltpu.VMEM((nd, chains, width), bf16),
+            pltpu.SemaphoreType.DMA((9,)),
             pltpu.SemaphoreType.DMA((nd,)),
             pltpu.SemaphoreType.DMA((copies,)),
             pltpu.SemaphoreType.DMA((copies,)),
@@ -666,7 +701,7 @@
         fault_pairs.T, fault_mult.reshape(-1, LANES),
     )
     theta_next, grad, pressure = pl.pallas_call(
-        finish_kernel,
+        functools.partial(finish_kernel, nm),
         out_shape=(
             jax.ShapeDtypeStruct((chains, modes_n), f32),
             jax.ShapeDtypeStruct((chains, modes_n), f32),
@@ -682,7 +717,8 @@
     share = theta.shape[1] // lax.axis_size("modes")
     nx = lax.axis_size("cells")
     whole = basis.shape[0] == NY * NZ and rest[-2].shape[0] % LANES == 0 and 2 * NZ == LANES
-    if share == nx and nx == 8 and whole and basis.shape[1] % (nx * LANES) == 0:
+    paired = lax.axis_size("modes") % 2 == 0 and 3 * rest[-2].shape[0] // LANES <= basis.shape[0] // LANES
+    if paired and share == nx and nx == 8 and whole and basis.shape[1] % (nx * LANES) == 0:
         return fast_body(theta, basis, *rest)
     return body(theta, basis, *rest)
 

time: 45.9 us -> 42.6 us (0.928)
  Pallas kernels: 45.1 us -> 41.8 us
    pallas_call x2, Pallas kernels: 45.1 us -> 41.8 us  [the longest x1 39.8 us: fast_body(): pl.pallas_call(functools.partial(fused_kernel, nd, nm, rows, parts, ('cel...]
where the time goes in v1:
time: 42.6 us; the launch traced here: 42.4 us
  Pallas kernels  41.8 us (98%)
  between operations  0.64 us (2%)
    pallas_call x1, Pallas kernels, fast_body(): pl.pallas_call(functools.partial(fused_kernel, nd, nm, rows, parts, ('cel...  39.8 us
    pallas_call x1, Pallas kernels, fast_body(): pl.pallas_call(functools.partial(finish_kernel, nm), out_shape=(jax.Shape...  1.99 us

profile of v1, /device:TPU:0, one launch (start us, length us, event | category | flops | bytes accessed | tf_op | source)
XLA Modules:
  0.0 42.4 jit_solution(17611967223707792622)
XLA Ops:
  0.6 39.8 %shard_map.130 = (bf16[8,32,256]{2,1,0:T(8,128)(2,1)}, f32[128,128]{1,0:T(8,128)}) custom-call(f32[32,2048]{1,0:T(8,128)} %bitcast.11, bf16[2048,2048]{1,0:T(8,128)(2,1)} %basis_hbm.1, f32[16,128]{1,0:T(8,128)} %bitcast.14, f32[3,2048]{1,0:T(4,128)} %face_hbm.1, f32[16,128]{1,0:T(8,128)} %bitcast.15, f32[16,128]{1,0:T(8,128)} %bitcast.16, ...), custom_call_target="tpu_custom_call" | custom-call | tf_op jit(solution)/shard_map/pallas_call | solution.py:659
  40.4 2.0 %shard_map.131 = (f32[32,2048]{1,0:T(8,128)}, f32[32,2048]{1,0:T(8,128)}, f32[8,2048]{1,0:T(8,128)}) custom-call(bf16[8,32,256]{2,1,0:T(8,128)(2,1)} %get-tuple-element.8.grad_ref, f32[128,128]{1,0:T(8,128)} %get-tuple-element.9.pres_ref, f32[32,2048]{1,0:T(8,128)} %bitcast.12, f32[32,2048]{1,0:T(8,128)} %bitcast.13), custom_call_target="tpu_custom_call" | custom-call | tf_op jit(solution)/shard_map/pallas_call | solution.py:703

commit v2 on v1

--- a/solution.py
+++ b/solution.py
@@ -285,27 +285,27 @@
     def bwd_lane(v, s):
         return pltpu.roll(v, s, 1)
 
-    def halves(vs):
-        return [pltpu.roll(v, NZ, 1) for v in vs]
-
-    def up_y(vs, hs):
+    fwd_low = [((lane + s) & (LANES - 1)) < NZ for s in range(4)]
+    bwd_low = [((lane - s) & (LANES - 1)) < NZ for s in range(4)]
+
+    def up_y(vs, s, hs=None):
         n = len(vs)
-        return [jnp.where(low, hs[r], hs[(r + 1) % n]) for r in range(n)]
-
-    def down_y(vs, hs):
+        hs = [pltpu.roll(v, NZ - s, 1) for v in vs] if hs is None else hs
+        return [jnp.where(fwd_low[s], hs[r], hs[(r + 1) % n]) for r in range(n)]
+
+    def down_y(vs, s, hs=None):
         n = len(vs)
-        return [jnp.where(low, hs[r - 1], hs[r]) for r in range(n)]
-
-    def ahead(vs, hs=None):
-        hs = halves(vs) if hs is None else hs
-        wy = up_y(vs, hs)
+        hs = [pltpu.roll(v, NZ + s, 1) for v in vs] if hs is None else hs
+        return [jnp.where(bwd_low[s], hs[r - 1], hs[r]) for r in range(n)]
+
+    def ahead(vs):
         return (
             [pltpu.roll(v, nx - 1, 0) for v in vs],
-            wy,
+            up_y(vs, 0),
             [fwd_lane(v, 1) for v in vs],
-            [fwd_lane(w, 1) for w in wy],
-            [fwd_lane(w, 2) for w in wy],
-            [fwd_lane(w, 3) for w in wy],
+            up_y(vs, 1),
+            up_y(vs, 2),
+            up_y(vs, 3),
         )
 
     def behind_one(kind, vs):
@@ -313,8 +313,7 @@
             return [pltpu.roll(v, 1, 0) for v in vs]
         if kind == 2:
             return [bwd_lane(v, 1) for v in vs]
-        wy = down_y(vs, halves(vs))
-        return wy if kind == 1 else [bwd_lane(w, kind - 2) for w in wy]
+        return down_y(vs, max(kind - 2, 0))
 
     every = range(rows)
     perm = [jnp.exp(logk_of(r)) for r in every]
@@ -355,18 +354,18 @@
             coef[k, r] = coef[k, r] * inv[r]
 
     def sweep(d):
-        hs = halves(d)
-        up = up_y(d, hs)
-        dn = down_y(d, hs)
+        hs = [pltpu.roll(v, NZ, 1) for v in d]
+        ups = [up_y(d, 0, hs)] + [up_y(d, s) for s in (1, 2, 3)]
+        dns = [down_y(d, 0, hs)] + [down_y(d, s) for s in (1, 2, 3)]
         out = []
         for r in every:
             v = d[r]
             acc = coef[0, r] * pltpu.roll(v, nx - 1, 0) + coef[1, r] * pltpu.roll(v, 1, 0)
-            acc2 = coef[2, r] * up[r] + coef[3, r] * dn[r]
-            acc = acc + coef[4, r] * fwd_lane(v, 1) + coef[5, r] * bwd_lane(v, 1)
+            acc2 = coef[2, r] * ups[0][r] + coef[3, r] * dns[0][r]
+            acc = acc + (coef[4, r] * fwd_lane(v, 1) + coef[5, r] * bwd_lane(v, 1))
             for s in (1, 2, 3):
-                acc2 = acc2 + coef[4 + 2 * s, r] * fwd_lane(up[r], s)
-                acc = acc + coef[5 + 2 * s, r] * bwd_lane(dn[r], s)
+                acc2 = acc2 + coef[4 + 2 * s, r] * ups[s][r]
+                acc = acc + coef[5 + 2 * s, r] * dns[s][r]
             out.append(acc + acc2)
         return out
 
@@ -427,7 +426,8 @@
         )
         for k in range(nd)
     ]
-    for load in small + loads:
+    flight = nd // 2
+    for load in small + loads[:flight]:
         load.start()
 
     def block(i, size):
@@ -491,34 +491,37 @@
     )
     stat[core, block(me, srows), :] = own_stat[core]
     share = chains // nm
-    theta_t = jnp.concatenate(
+    theta_b = jnp.concatenate(
         [
             theta_v[(2 * x + c) * share : (2 * x + c + 1) * share, :]
             for c in range(2)
             for x in range(pairs_n)
         ],
         0,
-    ).T.astype(jnp.bfloat16)
+    ).astype(jnp.bfloat16)
     half = rows // 2
-    lead = 1
     stat_got, part_got = [], []
-    for k in range(nd):
-        loads[k].wait()
-        got = jnp.dot(
-            basis[pl.ds(k * blk, blk), :], theta_t, preferred_element_type=jnp.float32
-        ).T
-        for t in range(blk // LANES):
+    for k in range(0, nd, 2):
+        for load in (k, k + 1):
+            loads[load].wait()
+            if load + flight < nd:
+                loads[load + flight].start()
+        got = lax.dot_general(
+            theta_b, basis[k * blk : (k + 2) * blk, :], (((1,), (1,)), ((), ())),
+            preferred_element_type=jnp.float32,
+        )
+        for t in range(2 * blk // LANES):
             r = k * (blk // LANES) + t
             part[r // half, pl.ds(r % half, chains, stride=half), :] = (
                 got[:, t * LANES : (t + 1) * LANES]
             )
-        if k == lead - 1:
+        if k == 0:
             pl.semaphore_wait(barrier, greeted)
             stat_got = [
                 send(own_stat.at[core], stat.at[core, block(me, srows)], cell_peer(t))
                 for t in near
             ]
-        if (k + 1) % (nd // 2) == 0:
+        if (k + 2) % (nd // 2) == 0:
             h = k // (nd // 2)
             part_got.append(
                 send(part.at[h, block(1 - core, chains // 2 * half)], part_in.at[h], mate)
@@ -604,9 +607,11 @@
         )
 
     g_got = []
-    for k, t in enumerate(near):
-        gsend[k] = piece(cell_of(t)).astype(jnp.bfloat16)
-        g_got.append(send(gsend.at[k], gin.at[k], cell_peer(t)))
+    for first, last in ((0, nd // 2), (nd // 2, nd - 1)):
+        for k in range(first, last):
+            gsend[k] = piece(cell_of(near[k])).astype(jnp.bfloat16)
+        for k in range(first, last):
+            g_got.append(send(gsend.at[k], gin.at[k], cell_peer(near[k])))
     grad = piece(me)
     for k, copy in enumerate(g_got):
         copy.wait_recv()

time: 42.6 us -> 41.3 us (0.969)
  Pallas kernels: 41.8 us -> 40.5 us
    pallas_call x1, Pallas kernels: 39.8 us -> 38.5 us  [fast_body(): pl.pallas_call(functools.partial(fused_kernel, nd, nm, rows, parts, ('cel...]
where the time goes in v2:
time: 41.3 us; the launch traced here: 41.2 us
  Pallas kernels  40.5 us (98%)
  between operations  0.64 us (2%)
    pallas_call x1, Pallas kernels, fast_body(): pl.pallas_call(functools.partial(fused_kernel, nd, nm, rows, parts, ('cel...  38.5 us
    pallas_call x1, Pallas kernels, fast_body(): pl.pallas_call(functools.partial(finish_kernel, nm), out_shape=(jax.Shape...  1.99 us

profile of v2, /device:TPU:0, one launch (start us, length us, event | category | flops | bytes accessed | tf_op | source)
XLA Modules:
  0.0 41.2 jit_solution(10794755606605652447)
XLA Ops:
  0.6 38.5 %shard_map.130 = (bf16[8,32,256]{2,1,0:T(8,128)(2,1)}, f32[128,128]{1,0:T(8,128)}) custom-call(f32[32,2048]{1,0:T(8,128)} %bitcast.11, bf16[2048,2048]{1,0:T(8,128)(2,1)} %basis_hbm.1, f32[16,128]{1,0:T(8,128)} %bitcast.14, f32[3,2048]{1,0:T(4,128)} %face_hbm.1, f32[16,128]{1,0:T(8,128)} %bitcast.15, f32[16,128]{1,0:T(8,128)} %bitcast.16, ...), custom_call_target="tpu_custom_call" | custom-call | tf_op jit(solution)/shard_map/pallas_call | solution.py:664
  39.2 2.0 %shard_map.131 = (f32[32,2048]{1,0:T(8,128)}, f32[32,2048]{1,0:T(8,128)}, f32[8,2048]{1,0:T(8,128)}) custom-call(bf16[8,32,256]{2,1,0:T(8,128)(2,1)} %get-tuple-element.8.grad_ref, f32[128,128]{1,0:T(8,128)} %get-tuple-element.9.pres_ref, f32[32,2048]{1,0:T(8,128)} %bitcast.12, f32[32,2048]{1,0:T(8,128)} %bitcast.13), custom_call_target="tpu_custom_call" | custom-call | tf_op jit(solution)/shard_map/pallas_call | solution.py:708

commit v3 on v2

--- a/solution.py
+++ b/solution.py
@@ -232,7 +232,7 @@
 
 
 LANES = 128
-STAT = 4
+STAT = 3
 
 
 def chebyshev(rhs, inv, sweep):
@@ -254,22 +254,28 @@
     return [a + b for a, b in zip(iterate, direction)]
 
 
-def chain_physics(nx, rows, logk_of, static_of, fault_row, parts, fault_s, coef, pres_s, before_fields, after_pressure, glogk_s):
+def chain_physics(nx, rows, logk_of, static_of, fault_row, parts, fault_s, coef, pres_s, before_fields, before_solve, after_pressure, glogk_s):
     hi_iota = lax.broadcasted_iota(jnp.int32, (rows, LANES), 0)
     lo_iota = lax.broadcasted_iota(jnp.int32, (LANES, LANES), 0)
     for x in range(nx):
-        got = None
+        lefts, los = [], []
         for part in range(parts):
             near = fault_row(x, part).astype(jnp.int32)
             shift = fault_row(x, parts + part).astype(jnp.int32) - near - NZ
-            lo = (lo_iota == (near & (LANES - 1))).astype(jnp.float32)
+            los.append((lo_iota == (near & (LANES - 1))).astype(jnp.bfloat16))
             hot = jnp.where(hi_iota == (near >> 7), fault_row(x, 2 * parts + part), 0.0)
-            left = jnp.concatenate([jnp.where(shift == s, hot, 0.0) for s in (1, 2, 3)], 0)
-            term = lax.dot_general(
-                left, lo, (((1,), (1,)), ((), ())),
-                precision=lax.Precision.HIGHEST, preferred_element_type=jnp.float32,
-            )
-            got = term if got is None else got + term
+            rest = [jnp.where(shift == s, hot, 0.0) for s in (1, 2, 3)]
+            pieces = []
+            for _ in range(3):
+                top = [v.astype(jnp.bfloat16) for v in rest]
+                rest = [v - t.astype(jnp.float32) for v, t in zip(rest, top)]
+                pieces += top
+            lefts.append(jnp.concatenate(pieces, 0))
+        got = lax.dot_general(
+            jnp.concatenate(lefts, 1), jnp.concatenate(los, 1), (((1,), (1,)), ((), ())),
+            preferred_element_type=jnp.float32,
+        )
+        got = (got[: 3 * rows] + got[3 * rows : 6 * rows]) + got[6 * rows :]
         for s in range(3):
             fault_s[s, pl.ds(x * rows, rows), :] = got[s * rows : (s + 1) * rows]
 
@@ -369,6 +375,7 @@
             out.append(acc + acc2)
         return out
 
+    before_solve()
     pres = chebyshev([static_of(4, r) for r in every], inv, sweep)
     for r in every:
         pres_s[pl.ds(r, nx, stride=rows), :] = pres[r]
@@ -395,7 +402,7 @@
     theta_hbm, basis_hbm, mean_hbm, face_hbm, storage_hbm, sources_hbm, data_hbm, weight_hbm,
     pairs_hbm, mult_hbm,
     grad_out, pres_out,
-    basis, theta_v, mean_v, face_v, pairs_v, mult_v, own_stat, stat, part, part_in, mine, field,
+    basis, theta_v, mean_v, face_v, pairs_v, mult_v, own_stat, own_late, stat, late, part, part_in, mine, field,
     fault_s, coef, pres_s, pres_in, glogk_s, gl_b, gl_all, gl_f, gsend, gin, gfin, gall,
     load_sem, copy_sem, send_sem, recv_sem,
 ):
@@ -411,10 +418,10 @@
     small = [
         (theta_hbm, theta_v),
         (face_hbm, face_v),
-        (storage_hbm, own_stat.at[0, pl.ds(3 * rows, rows)]),
-        (sources_hbm, own_stat.at[1, pl.ds(0, rows)]),
-        (data_hbm, own_stat.at[1, pl.ds(rows, rows)]),
-        (weight_hbm, own_stat.at[1, pl.ds(2 * rows, rows)]),
+        (storage_hbm, own_stat.at[1, pl.ds(0, rows)]),
+        (sources_hbm, own_stat.at[1, pl.ds(rows, rows)]),
+        (data_hbm, own_late.at[0]),
+        (weight_hbm, own_late.at[1]),
         (pairs_hbm, pairs_v),
         (mult_hbm, mult_v),
         (mean_hbm, mean_v),
@@ -483,13 +490,14 @@
         )
     pairs = pairs_v[...].astype(jnp.float32)
     spare = rows - 3 * parts
-    own_stat[1, 3 * rows :, :] = jnp.concatenate(
+    own_stat[1, 2 * rows :, :] = jnp.concatenate(
         [pairs[e : e + 1, p * LANES : (p + 1) * LANES] for e in range(2) for p in range(parts)]
         + [mult_v[...]]
         + ([jnp.zeros((spare, LANES), jnp.float32)] if spare else []),
         0,
     )
     stat[core, block(me, srows), :] = own_stat[core]
+    late[core, block(me, rows), :] = own_late[core]
     share = chains // nm
     theta_b = jnp.concatenate(
         [
@@ -541,6 +549,9 @@
         for t, dx in wide
     ]
     field[group, block(me, rows), :] = mine[group * nd + me]
+    late_got = [
+        send(own_late.at[core], late.at[core, block(me, rows)], cell_peer(t)) for t in near
+    ]
     for copy in stat_got:
         copy.wait_recv()
     send(stat.at[core], stat.at[core], mate).wait_recv()
@@ -550,6 +561,8 @@
             copy.wait_recv()
 
     def static_of(f, r):
+        if f > STAT + 1:
+            return late[f - STAT - 2, pl.ds(r, nd, stride=rows), :]
         h, f = (0, f) if f < STAT else (1, f - STAT)
         return stat[h, pl.ds(f * rows + r, nd, stride=srows), :]
 
@@ -560,9 +573,14 @@
         return value
 
     def fault_row(x, k):
-        return stat[1, pl.ds(x * srows + 3 * rows + k, 1), :]
-
-    pres_got = []
+        return stat[1, pl.ds(x * srows + 2 * rows + k, 1), :]
+
+    pres_got, swapped = [], []
+
+    def before_solve():
+        for copy in late_got:
+            copy.wait_recv()
+        swapped.append(send(late.at[core], late.at[core], mate))
 
     def after_pressure():
         for t in near:
@@ -572,10 +590,11 @@
                 )
             )
         pres_in[block(me, rows), :] = pres_s[block(me, rows), :]
+        swapped[0].wait_recv()
 
     chain_physics(
         nd, rows, logk_of, static_of, fault_row, parts, fault_s, coef, pres_s, before_fields,
-        after_pressure, glogk_s,
+        before_solve, after_pressure, glogk_s,
     )
 
     gl_b[...] = glogk_s[...].astype(jnp.bfloat16)
@@ -659,7 +678,7 @@
     f32, bf16 = jnp.float32, jnp.bfloat16
     width = modes_n // nd
     pairs_n = nm // 2
-    copies = 4 * (nd - 1) + 2 * (pairs_n * nd - 1) + 4
+    copies = 5 * (nd - 1) + 2 * (pairs_n * nd - 1) + 5
     vmem = pl.BlockSpec(memory_space=pltpu.VMEM)
     grad, pressure = pl.pallas_call(
         functools.partial(fused_kernel, nd, nm, rows, parts, ("cells", "modes")),
@@ -677,7 +696,9 @@
             pltpu.VMEM((2, parts * LANES), jnp.int32),
             pltpu.VMEM((parts, LANES), f32),
             pltpu.VMEM((2, STAT * rows, LANES), f32),
+            pltpu.VMEM((2, rows, LANES), f32),
             pltpu.VMEM((2, nd * STAT * rows, LANES), f32),
+            pltpu.VMEM((2, nd * rows, LANES), f32),
             pltpu.VMEM((2, chains * rows // 2, LANES), f32),
             pltpu.VMEM((2, chains // 2 * rows // 2, LANES), f32),
             pltpu.VMEM((pairs_n * nd, rows, LANES), f32),
@@ -699,11 +720,11 @@
             pltpu.SemaphoreType.DMA((copies,)),
             pltpu.SemaphoreType.DMA((copies,)),
         ],
-        compiler_params=pltpu.CompilerParams(collective_id=0, has_side_effects=True),
+        compiler_params=pltpu.CompilerParams(collective_id=0, has_side_effects=True, vmem_limit_bytes=24 << 20),
     )(
-        theta.T, basis, mean_logk.reshape(-1, LANES), face_mult, storage.reshape(-1, LANES),
+        *[pltpu.with_memory_space_constraint(a, pltpu.HBM) for a in (theta.T, basis, mean_logk.reshape(-1, LANES), face_mult, storage.reshape(-1, LANES),
         sources.reshape(-1, LANES), obs_data.reshape(-1, LANES), obs_weight.reshape(-1, LANES),
-        fault_pairs.T, fault_mult.reshape(-1, LANES),
+        fault_pairs.T, fault_mult.reshape(-1, LANES))],
     )
     theta_next, grad, pressure = pl.pallas_call(
         functools.partial(finish_kernel, nm),
@@ -714,6 +735,7 @@
         ),
         in_specs=[vmem] * 4,
         out_specs=(vmem,) * 3,
+        compiler_params=pltpu.CompilerParams(vmem_limit_bytes=16 << 20),
     )(grad, pressure, theta.T, noise.T)
     return (theta_next.T, grad.T, pressure)
 

time: 41.3 us -> 38.3 us (0.927)
  Pallas kernels: 40.5 us -> 37.4 us
    pallas_call x1, Pallas kernels: 38.5 us -> 36.6 us  [fast_body(): pl.pallas_call(functools.partial(fused_kernel, nd, nm, rows, parts, ('cel...]
    pallas_call x1, Pallas kernels: 1.99 us -> 0.85 us  [fast_body(): pl.pallas_call(functools.partial(finish_kernel, nm), out_shape=(jax.Shape...]
where the time goes in v3:
time: 38.3 us; the launch traced here: 38.1 us
  Pallas kernels  37.4 us (98%)
  between operations  0.67 us (2%)
    pallas_call x1, Pallas kernels, fast_body(): pl.pallas_call(functools.partial(fused_kernel, nd, nm, rows, parts, ('cel...  36.6 us
    pallas_call x1, Pallas kernels, fast_body(): pl.pallas_call(functools.partial(finish_kernel, nm), out_shape=(jax.Shape...  0.85 us

profile of v3, /device:TPU:0, one launch (start us, length us, event | category | flops | bytes accessed | tf_op | source)
XLA Modules:
  0.0 38.1 jit_solution(419382245014600366)
XLA Ops:
  0.6 0.0 copy-start.1
  0.6 0.0 copy-start
  0.7 36.6 %shard_map.130 = (bf16[8,32,256]{2,1,0:T(8,128)(2,1)S(1)}, f32[128,128]{1,0:T(8,128)S(1)}) custom-call(f32[32,2048]{1,0:T(8,128)} %bitcast.11, bf16[2048,2048]{1,0:T(8,128)(2,1)} %basis_hbm.1, f32[16,128]{1,0:T(8,128)} %bitcast.14, f32[3,2048]{1,0:T(4,128)} %face_hbm.1, f32[16,128]{1,0:T(8,128)} %bitcast.15, f32[16,128]{1,0:T(8,128)} %bitcast.16, ...), custom_call_target="tpu_custom_call" | custom-call | tf_op jit(solution)/shard_map/pallas_call | solution.py:683
  37.2 0.0 copy-done.1
  37.2 0.0 copy-done
  37.3 0.9 %shard_map.131 = (f32[32,2048]{1,0:T(8,128)}, f32[32,2048]{1,0:T(8,128)}, f32[8,2048]{1,0:T(8,128)}) custom-call(bf16[8,32,256]{2,1,0:T(8,128)(2,1)S(1)} %get-tuple-element.8.grad_ref, f32[128,128]{1,0:T(8,128)S(1)} %get-tuple-element.9.pres_ref, f32[32,2048]{1,0:T(8,128)S(1)} %bitcast.12, f32[32,2048]{1,0:T(8,128)S(1)} %bitcast.13), custom_call_target="tpu_custom_call" | custom-call | tf_op jit(solution)/shard_map/pallas_call | solution.py:729
Async XLA Ops:
  0.6 36.6 %copy-start.1 = (f32[2048,32]{0,1:T(8,128)S(1)}, f32[2048,32]{0,1:T(8,128)}, u32[]{:S(2)}) copy-start(f32[2048,32]{0,1:T(8,128)} %param.21) | copy-start | bytes 786436
  0.6 36.6 %copy-start = (f32[2048,32]{0,1:T(8,128)S(1)}, f32[2048,32]{0,1:T(8,128)}, u32[]{:S(2)}) copy-start(f32[2048,32]{0,1:T(8,128)} %param.11) | copy-start | bytes 786436

commit v4 on v3

--- a/solution.py
+++ b/solution.py
@@ -254,7 +254,7 @@
     return [a + b for a, b in zip(iterate, direction)]
 
 
-def chain_physics(nx, rows, logk_of, static_of, fault_row, parts, fault_s, coef, pres_s, before_fields, before_solve, after_pressure, glogk_s):
+def chain_physics(nx, rows, logk_of, static_of, fault_row, parts, fault_s, coef, pres_s, before_fields, before_misfit, glogk_s):
     hi_iota = lax.broadcasted_iota(jnp.int32, (rows, LANES), 0)
     lo_iota = lax.broadcasted_iota(jnp.int32, (LANES, LANES), 0)
     for x in range(nx):
@@ -375,11 +375,10 @@
             out.append(acc + acc2)
         return out
 
-    before_solve()
     pres = chebyshev([static_of(4, r) for r in every], inv, sweep)
     for r in every:
         pres_s[pl.ds(r, nx, stride=rows), :] = pres[r]
-    after_pressure()
+    before_misfit()
     misfit = [static_of(6, r) * (pres[r] - static_of(5, r)) for r in every]
     adj = chebyshev(misfit, inv, sweep)
     pres_a = ahead(pres)
@@ -497,7 +496,7 @@
         0,
     )
     stat[core, block(me, srows), :] = own_stat[core]
-    late[core, block(me, rows), :] = own_late[core]
+    late[:, block(me, rows), :] = own_late[...]
     share = chains // nm
     theta_b = jnp.concatenate(
         [
@@ -550,7 +549,7 @@
     ]
     field[group, block(me, rows), :] = mine[group * nd + me]
     late_got = [
-        send(own_late.at[core], late.at[core, block(me, rows)], cell_peer(t)) for t in near
+        send(own_late, late.at[:, block(me, rows)], cell_peer(t)) for t in near
     ]
     for copy in stat_got:
         copy.wait_recv()
@@ -575,26 +574,13 @@
     def fault_row(x, k):
         return stat[1, pl.ds(x * srows + 2 * rows + k, 1), :]
 
-    pres_got, swapped = [], []
-
-    def before_solve():
+    def before_misfit():
         for copy in late_got:
             copy.wait_recv()
-        swapped.append(send(late.at[core], late.at[core], mate))
-
-    def after_pressure():
-        for t in near:
-            pres_got.append(
-                send(
-                    pres_s.at[block(cell_of(t), rows)], pres_in.at[block(me, rows)], cell_peer(t)
-                )
-            )
-        pres_in[block(me, rows), :] = pres_s[block(me, rows), :]
-        swapped[0].wait_recv()
 
     chain_physics(
         nd, rows, logk_of, static_of, fault_row, parts, fault_s, coef, pres_s, before_fields,
-        before_solve, after_pressure, glogk_s,
+        before_misfit, glogk_s,
     )
 
     gl_b[...] = glogk_s[...].astype(jnp.bfloat16)
@@ -604,12 +590,14 @@
         for t, dx in wide
     ]
     gl_all[core, spot, :] = gl_b[block(me, rows), :]
+    pres_got = [
+        send(pres_s.at[block(cell_of(t), rows)], pres_in.at[block(me, rows)], cell_peer(t))
+        for t in near
+    ]
+    pres_in[block(me, rows), :] = pres_s[block(me, rows), :]
     for copy in gl_got:
         copy.wait_recv()
     mate_got = send(gl_all.at[core], gl_all.at[core], mate)
-    for copy in pres_got:
-        copy.wait_recv()
-    pres_out[...] = pres_in[...]
     mate_got.wait_recv()
     held = chains // 2 * rows
     for c in range(2):
@@ -626,7 +614,7 @@
         )
 
     g_got = []
-    for first, last in ((0, nd // 2), (nd // 2, nd - 1)):
+    for first, last in ((0, 2), (2, 4), (4, nd - 1)):
         for k in range(first, last):
             gsend[k] = piece(cell_of(near[k])).astype(jnp.bfloat16)
         for k in range(first, last):
@@ -638,10 +626,15 @@
     gfin[...] = grad.astype(jnp.bfloat16)
     g_got = [send(gfin, gall.at[me], cell_peer(t)) for t in near]
     gall[me] = gfin[...]
+    for copy in pres_got:
+        copy.wait_recv()
+    pres_out[...] = pres_in[...]
+    for copy in sent[: -len(near)]:
+        copy.wait_send()
     for copy in g_got:
         copy.wait_recv()
     grad_out[...] = gall[...]
-    for copy in sent:
+    for copy in sent[-len(near) :]:
         copy.wait_send()
 
 
@@ -678,7 +671,7 @@
     f32, bf16 = jnp.float32, jnp.bfloat16
     width = modes_n // nd
     pairs_n = nm // 2
-    copies = 5 * (nd - 1) + 2 * (pairs_n * nd - 1) + 5
+    copies = 5 * (nd - 1) + 2 * (pairs_n * nd - 1) + 4
     vmem = pl.BlockSpec(memory_space=pltpu.VMEM)
     grad, pressure = pl.pallas_call(
         functools.partial(fused_kernel, nd, nm, rows, parts, ("cells", "modes")),

time: 38.3 us -> 37.9 us (0.990)
  Pallas kernels: 37.4 us -> 37 us
    pallas_call x1, Pallas kernels: 36.6 us -> 36.2 us  [fast_body(): pl.pallas_call(functools.partial(fused_kernel, nd, nm, rows, parts, ('cel...]
where the time goes in v4:
time: 37.9 us; the launch traced here: 37.7 us
  Pallas kernels  37 us (98%)
  between operations  0.67 us (2%)
    pallas_call x1, Pallas kernels, fast_body(): pl.pallas_call(functools.partial(fused_kernel, nd, nm, rows, parts, ('cel...  36.2 us
    pallas_call x1, Pallas kernels, fast_body(): pl.pallas_call(functools.partial(finish_kernel, nm), out_shape=(jax.Shape...  0.85 us

profile of v4, /device:TPU:0, one launch (start us, length us, event | category | flops | bytes accessed | tf_op | source)
XLA Modules:
  0.0 37.7 jit_solution(2551724839080472779)
XLA Ops:
  0.6 0.0 copy-start.1
  0.6 0.0 copy-start
  0.7 36.2 %shard_map.130 = (bf16[8,32,256]{2,1,0:T(8,128)(2,1)S(1)}, f32[128,128]{1,0:T(8,128)S(1)}) custom-call(f32[32,2048]{1,0:T(8,128)} %bitcast.11, bf16[2048,2048]{1,0:T(8,128)(2,1)} %basis_hbm.1, f32[16,128]{1,0:T(8,128)} %bitcast.14, f32[3,2048]{1,0:T(4,128)} %face_hbm.1, f32[16,128]{1,0:T(8,128)} %bitcast.15, f32[16,128]{1,0:T(8,128)} %bitcast.16, ...), custom_call_target="tpu_custom_call" | custom-call | tf_op jit(solution)/shard_map/pallas_call | solution.py:676
  36.8 0.0 copy-done.1
  36.9 0.0 copy-done
  36.9 0.9 %shard_map.131 = (f32[32,2048]{1,0:T(8,128)}, f32[32,2048]{1,0:T(8,128)}, f32[8,2048]{1,0:T(8,128)}) custom-call(bf16[8,32,256]{2,1,0:T(8,128)(2,1)S(1)} %get-tuple-element.8.grad_ref, f32[128,128]{1,0:T(8,128)S(1)} %get-tuple-element.9.pres_ref, f32[32,2048]{1,0:T(8,128)S(1)} %bitcast.12, f32[32,2048]{1,0:T(8,128)S(1)} %bitcast.13), custom_call_target="tpu_custom_call" | custom-call | tf_op jit(solution)/shard_map/pallas_call | solution.py:722
Async XLA Ops:
  0.6 36.2 %copy-start.1 = (f32[2048,32]{0,1:T(8,128)S(1)}, f32[2048,32]{0,1:T(8,128)}, u32[]{:S(2)}) copy-start(f32[2048,32]{0,1:T(8,128)} %param.21) | copy-start | bytes 786436
  0.6 36.2 %copy-start = (f32[2048,32]{0,1:T(8,128)S(1)}, f32[2048,32]{0,1:T(8,128)}, u32[]{:S(2)}) copy-start(f32[2048,32]{0,1:T(8,128)} %param.11) | copy-start | bytes 786436

commit v5 on v4

--- a/solution.py
+++ b/solution.py
@@ -378,20 +378,23 @@
     pres = chebyshev([static_of(4, r) for r in every], inv, sweep)
     for r in every:
         pres_s[pl.ds(r, nx, stride=rows), :] = pres[r]
+    pres_a = ahead(pres)
+    perm_a = ahead(perm)
+    for k in range(6):
+        for r in every:
+            drop = (pres[r] - pres_a[k][r]) * coef[12 + k, r]
+            coef[12 + k, r] = drop * perm_a[k][r]
+            coef[18 + k, r] = drop * perm[r]
     before_misfit()
     misfit = [static_of(6, r) * (pres[r] - static_of(5, r)) for r in every]
     adj = chebyshev(misfit, inv, sweep)
-    pres_a = ahead(pres)
     adj_a = ahead(adj)
-    perm_a = ahead(perm)
     total = [zero for r in every]
     for k in range(6):
-        q = [
-            -(adj[r] - adj_a[k][r]) * (pres[r] - pres_a[k][r]) * coef[12 + k, r] for r in every
-        ]
-        back = behind_one(k, [q[r] * perm[r] for r in every])
+        rise = [adj_a[k][r] - adj[r] for r in every]
+        back = behind_one(k, [rise[r] * coef[18 + k, r] for r in every])
         for r in every:
-            total[r] = total[r] + q[r] * perm_a[k][r] + back[r]
+            total[r] = total[r] + rise[r] * coef[12 + k, r] + back[r]
     for r in every:
         glogk_s[pl.ds(r, nx, stride=rows), :] = total[r]
 
@@ -399,11 +402,11 @@
 def fused_kernel(
     nd, nm, rows, parts, axes,
     theta_hbm, basis_hbm, mean_hbm, face_hbm, storage_hbm, sources_hbm, data_hbm, weight_hbm,
-    pairs_hbm, mult_hbm,
-    grad_out, pres_out,
-    basis, theta_v, mean_v, face_v, pairs_v, mult_v, own_stat, own_late, stat, late, part, part_in, mine, field,
+    pairs_hbm, mult_hbm, noise_hbm,
+    grad_out, pres_out, drift_out,
+    basis, theta_v, noise_v, mean_v, face_v, pairs_v, mult_v, own_stat, own_late, stat, late, part, part_in, mine, field,
     fault_s, coef, pres_s, pres_in, glogk_s, gl_b, gl_all, gl_f, gsend, gin, gfin, gall,
-    load_sem, copy_sem, send_sem, recv_sem,
+    load_sem, copy_sem, noise_sem, send_sem, recv_sem,
 ):
     cells_ax, modes_ax = axes
     me, mo = lax.axis_index(cells_ax), lax.axis_index(modes_ax)
@@ -441,7 +444,7 @@
 
     steps = sorted(
         ((dz, dy) for dz in range(nd // 2) for dy in range(2)),
-        key=lambda t: -(min(t[0], nd // 2 - t[0]) + t[1]),
+        key=lambda t: -(min(t[0], nd // 2 - t[0]) + 2 * t[1]),
     )
 
     def cell_of(step):
@@ -450,7 +453,7 @@
     near = [t for t in steps if t != (0, 0)]
     wide = sorted(
         ((t, dx) for t in steps for dx in range(pairs_n) if (t, dx) != ((0, 0), 0)),
-        key=lambda w: -(min(w[0][0], nd // 2 - w[0][0]) + w[0][1] + (w[1] > 0)),
+        key=lambda w: -(min(w[0][0], nd // 2 - w[0][0]) + 2 * w[0][1] + 2 * (w[1] > 0)),
     )
     mate = {modes_ax: group * 2 + 1 - core}
 
@@ -533,6 +536,8 @@
             part_got.append(
                 send(part.at[h, block(1 - core, chains // 2 * half)], part_in.at[h], mate)
             )
+    noise_load = pltpu.make_async_copy(noise_hbm, noise_v, noise_sem)
+    noise_load.start()
     mean = 1.0 / pairs_n * mean_v[...]
     for h in range(2):
         total = part[h, block(core, chains // 2 * half), :].reshape(chains // 2, half, LANES)
@@ -595,6 +600,8 @@
         for t in near
     ]
     pres_in[block(me, rows), :] = pres_s[block(me, rows), :]
+    noise_load.wait()
+    drift_out[...] = (1.0 - STEP_SIZE) * theta_v[...] + math.sqrt(2.0 * STEP_SIZE) * noise_v[...]
     for copy in gl_got:
         copy.wait_recv()
     mate_got = send(gl_all.at[core], gl_all.at[core], mate)
@@ -638,25 +645,36 @@
         copy.wait_send()
 
 
-def finish_kernel(nm, grad_ref, pres_ref, theta_ref, noise_ref, theta_out, grad_out, pres_out):
+def finish_kernel(
+    nm, grad_ref, pres_ref, drift_ref, theta_hbm, grad_hbm, pres_hbm, theta_v, grad_v, pres_v, sems
+):
     pieces, chains, width = grad_ref.shape
     share = chains // nm
     order = [x * 2 + c for c in range(2) for x in range(nm // 2)]
-    for p in range(pieces):
-        cols = slice(p * width, (p + 1) * width)
-        piece = grad_ref[p].astype(jnp.float32)
-        g = jnp.concatenate(
-            [piece[order.index(n) * share : (order.index(n) + 1) * share] for n in range(nm)], 0
-        )
-        t = theta_ref[:, cols]
-        grad_out[:, cols] = g
-        theta_out[:, cols] = (
-            t - STEP_SIZE * (g + t) + math.sqrt(2.0 * STEP_SIZE) * noise_ref[:, cols]
-        )
-    count = pres_out.shape[0]
-    rows = pres_out.shape[1] // LANES
+    count = pres_v.shape[0]
+    rows = pres_v.shape[1] // LANES
     for r in range(rows):
-        pres_out[:, r * LANES : (r + 1) * LANES] = pres_ref[pl.ds(r, count, stride=rows), :]
+        pres_v[:, r * LANES : (r + 1) * LANES] = pres_ref[pl.ds(r, count, stride=rows), :]
+    copies = [pltpu.make_async_copy(pres_v, pres_hbm, sems.at[0])]
+    copies[0].start()
+    group = pieces // 4
+    for q in range(4):
+        for p in range(q * group, (q + 1) * group):
+            cols = slice(p * width, (p + 1) * width)
+            piece = grad_ref[p].astype(jnp.float32)
+            g = jnp.concatenate(
+                [piece[order.index(n) * share : (order.index(n) + 1) * share] for n in range(nm)],
+                0,
+            )
+            grad_v[:, cols] = g
+            theta_v[:, cols] = drift_ref[:, cols] - STEP_SIZE * g
+        cols = pl.ds(q * group * width, group * width)
+        for i, (src, dst) in enumerate(((grad_v, grad_hbm), (theta_v, theta_hbm))):
+            copy = pltpu.make_async_copy(src.at[:, cols], dst.at[:, cols], sems.at[1 + 2 * q + i])
+            copy.start()
+            copies.append(copy)
+    for copy in copies:
+        copy.wait()
 
 
 def fast_body(
@@ -673,16 +691,18 @@
     pairs_n = nm // 2
     copies = 5 * (nd - 1) + 2 * (pairs_n * nd - 1) + 4
     vmem = pl.BlockSpec(memory_space=pltpu.VMEM)
-    grad, pressure = pl.pallas_call(
+    grad, pressure, drift = pl.pallas_call(
         functools.partial(fused_kernel, nd, nm, rows, parts, ("cells", "modes")),
         out_shape=(
             jax.ShapeDtypeStruct((nd, chains, width), bf16),
             jax.ShapeDtypeStruct((nd * rows, LANES), f32),
+            jax.ShapeDtypeStruct((chains, modes_n), f32),
         ),
-        in_specs=[pl.BlockSpec(memory_space=pl.ANY)] * 10,
-        out_specs=(vmem,) * 2,
+        in_specs=[pl.BlockSpec(memory_space=pl.ANY)] * 11,
+        out_specs=(vmem,) * 3,
         scratch_shapes=[
             pltpu.VMEM((cells, modes_n), bf16),
+            pltpu.VMEM((chains, modes_n), f32),
             pltpu.VMEM((chains, modes_n), f32),
             pltpu.VMEM((rows, LANES), f32),
             pltpu.VMEM((3, cells), f32),
@@ -697,7 +717,7 @@
             pltpu.VMEM((pairs_n * nd, rows, LANES), f32),
             pltpu.VMEM((pairs_n, nd * rows, LANES), f32),
             pltpu.VMEM((3, nd * rows, LANES), f32),
-            pltpu.VMEM((18, rows, nd, LANES), f32),
+            pltpu.VMEM((24, rows, nd, LANES), f32),
             pltpu.VMEM((nd * rows, LANES), f32),
             pltpu.VMEM((nd * rows, LANES), f32),
             pltpu.VMEM((nd * rows, LANES), f32),
@@ -710,6 +730,7 @@
             pltpu.VMEM((nd, chains, width), bf16),
             pltpu.SemaphoreType.DMA((9,)),
             pltpu.SemaphoreType.DMA((nd,)),
+            pltpu.SemaphoreType.DMA,
             pltpu.SemaphoreType.DMA((copies,)),
             pltpu.SemaphoreType.DMA((copies,)),
         ],
@@ -717,7 +738,7 @@
     )(
         *[pltpu.with_memory_space_constraint(a, pltpu.HBM) for a in (theta.T, basis, mean_logk.reshape(-1, LANES), face_mult, storage.reshape(-1, LANES),
         sources.reshape(-1, LANES), obs_data.reshape(-1, LANES), obs_weight.reshape(-1, LANES),
-        fault_pairs.T, fault_mult.reshape(-1, LANES))],
+        fault_pairs.T, fault_mult.reshape(-1, LANES), noise.T)],
     )
     theta_next, grad, pressure = pl.pallas_call(
         functools.partial(finish_kernel, nm),
@@ -726,10 +747,16 @@
             jax.ShapeDtypeStruct((chains, modes_n), f32),
             jax.ShapeDtypeStruct((chains // nm, cells), f32),
         ),
-        in_specs=[vmem] * 4,
-        out_specs=(vmem,) * 3,
+        in_specs=[vmem] * 3,
+        out_specs=(pl.BlockSpec(memory_space=pl.ANY),) * 3,
+        scratch_shapes=[
+            pltpu.VMEM((chains, modes_n), f32),
+            pltpu.VMEM((chains, modes_n), f32),
+            pltpu.VMEM((chains // nm, cells), f32),
+            pltpu.SemaphoreType.DMA((9,)),
+        ],
         compiler_params=pltpu.CompilerParams(vmem_limit_bytes=16 << 20),
-    )(grad, pressure, theta.T, noise.T)
+    )(grad, pressure, drift)
     return (theta_next.T, grad.T, pressure)
 
 

time: 37.9 us -> 37.7 us (level)
  no operation moved by 1% of the time
where the time goes in v5:
time: 37.7 us; the launch traced here: 37.6 us
  Pallas kernels  36.9 us (98%)
  between operations  0.64 us (2%)
    pallas_call x1, Pallas kernels, fast_body(): pl.pallas_call(functools.partial(fused_kernel, nd, nm, rows, parts, ('cel...  36 us
    pallas_call x1, Pallas kernels, fast_body(): pl.pallas_call(functools.partial(finish_kernel, nm), out_shape=(jax.Shape...  0.9 us

profile of v5, /device:TPU:0, one launch (start us, length us, event | category | flops | bytes accessed | tf_op | source)
XLA Modules:
  0.0 37.6 jit_solution(7183324976508402734)
XLA Ops:
  0.6 36.0 %shard_map.130 = (bf16[8,32,256]{2,1,0:T(8,128)(2,1)S(1)}, f32[128,128]{1,0:T(8,128)S(1)}, f32[32,2048]{1,0:T(8,128)S(1)}) custom-call(f32[32,2048]{1,0:T(8,128)} %bitcast.11, bf16[2048,2048]{1,0:T(8,128)(2,1)} %basis_hbm.1, f32[16,128]{1,0:T(8,128)} %bitcast.13, f32[3,2048]{1,0:T(4,128)} %face_hbm.1, f32[16,128]{1,0:T(8,128)} %bitcast.14, ...), custom_call_target="tpu_custom_call" | custom-call | tf_op jit(solution)/shard_map/pallas_call | solution.py:694
  36.7 0.9 %shard_map.131 = (f32[32,2048]{1,0:T(8,128)}, f32[32,2048]{1,0:T(8,128)}, f32[8,2048]{1,0:T(8,128)}) custom-call(bf16[8,32,256]{2,1,0:T(8,128)(2,1)S(1)} %get-tuple-element.9.grad_ref, f32[128,128]{1,0:T(8,128)S(1)} %get-tuple-element.10.pres_ref, f32[32,2048]{1,0:T(8,128)S(1)} %get-tuple-element.11.drift_ref), custom_call_target="tpu_custom_call" | custom-call | tf_op jit(solution)/shard_map/pallas_call | solution.py:743

commit v6 on v5

--- a/solution.py
+++ b/solution.py
@@ -602,10 +602,15 @@
     pres_in[block(me, rows), :] = pres_s[block(me, rows), :]
     noise_load.wait()
     drift_out[...] = (1.0 - STEP_SIZE) * theta_v[...] + math.sqrt(2.0 * STEP_SIZE) * noise_v[...]
-    for copy in gl_got:
+    mate_got = []
+    for dx in range(pairs_n):
+        for copy, (_, step) in zip(gl_got, wide):
+            if step == dx:
+                copy.wait_recv()
+        held_rows = block(lax.rem(group + pairs_n - dx, pairs_n), nd * rows)
+        mate_got.append(send(gl_all.at[core, held_rows], gl_all.at[core, held_rows], mate))
+    for copy in mate_got:
         copy.wait_recv()
-    mate_got = send(gl_all.at[core], gl_all.at[core], mate)
-    mate_got.wait_recv()
     held = chains // 2 * rows
     for c in range(2):
         gl_f[c * held : (c + 1) * held, :] = gl_all[c].astype(jnp.float32)
@@ -689,7 +694,7 @@
     f32, bf16 = jnp.float32, jnp.bfloat16
     width = modes_n // nd
     pairs_n = nm // 2
-    copies = 5 * (nd - 1) + 2 * (pairs_n * nd - 1) + 4
+    copies = 5 * (nd - 1) + 2 * (pairs_n * nd - 1) + 3 + pairs_n
     vmem = pl.BlockSpec(memory_space=pltpu.VMEM)
     grad, pressure, drift = pl.pallas_call(
         functools.partial(fused_kernel, nd, nm, rows, parts, ("cells", "modes")),

time: 37.7 us -> 37.7 us (level)
  no operation moved by 1% of the time
where the time goes in v6:
time: 37.7 us; the launch traced here: 37.6 us
  Pallas kernels  37 us (98%)
  between operations  0.64 us (2%)
    pallas_call x1, Pallas kernels, fast_body(): pl.pallas_call(functools.partial(fused_kernel, nd, nm, rows, parts, ('cel...  36 us
    pallas_call x1, Pallas kernels, fast_body(): pl.pallas_call(functools.partial(finish_kernel, nm), out_shape=(jax.Shape...  0.9 us

profile of v6, /device:TPU:0, one launch (start us, length us, event | category | flops | bytes accessed | tf_op | source)
XLA Modules:
  0.0 37.6 jit_solution(12245319333090892916)
XLA Ops:
  0.6 36.0 %shard_map.130 = (bf16[8,32,256]{2,1,0:T(8,128)(2,1)S(1)}, f32[128,128]{1,0:T(8,128)S(1)}, f32[32,2048]{1,0:T(8,128)S(1)}) custom-call(f32[32,2048]{1,0:T(8,128)} %bitcast.11, bf16[2048,2048]{1,0:T(8,128)(2,1)} %basis_hbm.1, f32[16,128]{1,0:T(8,128)} %bitcast.13, f32[3,2048]{1,0:T(4,128)} %face_hbm.1, f32[16,128]{1,0:T(8,128)} %bitcast.14, ...), custom_call_target="tpu_custom_call" | custom-call | tf_op jit(solution)/shard_map/pallas_call | solution.py:699
  36.7 0.9 %shard_map.131 = (f32[32,2048]{1,0:T(8,128)}, f32[32,2048]{1,0:T(8,128)}, f32[8,2048]{1,0:T(8,128)}) custom-call(bf16[8,32,256]{2,1,0:T(8,128)(2,1)S(1)} %get-tuple-element.9.grad_ref, f32[128,128]{1,0:T(8,128)S(1)} %get-tuple-element.10.pres_ref, f32[32,2048]{1,0:T(8,128)S(1)} %get-tuple-element.11.drift_ref), custom_call_target="tpu_custom_call" | custom-call | tf_op jit(solution)/shard_map/pallas_call | solution.py:748
